TPU v7x, 128 devices: a whole 4x4x4 slice. The times are simulated.
128 devices in a mesh: group: 8 (over x, core), sub: 16 (over z, y).
Axes of the slice: x: 4, y: 4, z: 4, core: 2. Of those that a mesh axis runs over, the one named last changes fastest.
Arguments:
- schur: bfloat16 [8, 16, 1024, 1024], P('group', 'sub'), as said below
- local_inverse: bfloat16 [8, 16, 1024, 1024], P('group', 'sub'), as said below
- rhs_parts: bfloat16 [8, 16, 1024, 128], P('group', 'sub'), may hold values from -6 to 6
- basis: bfloat16 [8, 16, 32, 1024], P('group', 'sub'), may hold values from -0.1875 to 0.1875
- coarse_map: int32 [8, 16, 32], P('group', 'sub'), may hold values from 0 to 1023
- coarse_inverse: bfloat16 [8, 1024, 1024], P('group', 'sub'), as said below
- shared_rows: int32 [8, 16, 2, 4, 256], P('group', 'sub'), may hold values from 0 to 1023, as said below
- shared_counts: int32 [8, 16, 4], P('group', 'sub'), may hold values from 0 to 256, as said below
Outputs:
- solution: float32 [8, 16, 1024, 128], P('group', 'sub')
- residual: float32 [8, 16, 1024, 128], P('group', 'sub')
Inputs may be any that keep to these rules, and one draw needn't show every extreme that they name: `schur`: each subdomain matrix is symmetric positive definite. `local_inverse`: each subdomain matrix is symmetric positive definite. `coarse_inverse`: each group's matrix is symmetric positive definite. `shared_rows`: own rows of direction d lie in rows d * 256 to (d + 1) * 256 - 1 and are distinct within a list; the own rows of direction 0 of (g, s) are the partner rows of direction 1 of (g, s + 1) and the reverse, likewise directions 2 and 3 between (g, s) and (g + 1, s); entries past the count are rows of the same block. `shared_counts`: the count of direction 0 of (g, s) equals the count of direction 1 of (g, s + 1), that of direction 2 of (g, s) the count of direction 3 of (g + 1, s); counts are 0 where no neighbour exists; some count equals 256.
All inputs are finite; a program needn't handle non-finite values.
Results may differ from a plain program's by a relative error of at most 0.014.
Values may be sent and summed in bfloat16 or wider, within the bound.
A program may use at most 64 MiB of HBM per device.

v0:
```python
import jax
import jax.numpy as jnp
from jax import lax
from jax.sharding import PartitionSpec as P

ITERS = 3


def extended(block, sides, width):
    for axis, dim in sides:
        count = lax.axis_size(axis)
        forward = [(i, i + 1) for i in range(count - 1)]
        backward = [(target, source) for source, target in forward]
        low = lax.ppermute(
            lax.slice_in_dim(block, block.shape[dim] - width, None, axis=dim), axis, forward
        )
        high = lax.ppermute(lax.slice_in_dim(block, 0, width, axis=dim), axis, backward)
        block = jnp.concatenate([low, block, high], axis=dim)
    return block


def pick_rows(tables, indices):
    return jax.vmap(jax.vmap(lambda source_block, rows_at: source_block[rows_at]))(tables, indices)


def add_rows(bases, indices, additions):

    def add_single(base_block, rows_at, extra):
        return base_block.at[rows_at.reshape(-1)].add(extra.reshape(-1, base_block.shape[-1]))

    return jax.vmap(jax.vmap(add_single))(bases, indices, additions)


def count_rows(indices, live_mask, rows_local):

    def count_single(rows_at, mask_rows):
        return (
            jnp.ones((rows_local,), jnp.float32).at[rows_at.reshape(-1)].add(mask_rows.reshape(-1))
        )

    return jax.vmap(jax.vmap(count_single))(indices, live_mask)


def assemble(blocks, own_rows, partner_rows, live_mask):
    padded = extended(blocks, (("group", 0), ("sub", 1)), 1)
    received = jnp.stack(
        [
            pick_rows(padded[1:2, 2:], partner_rows[:, :, 0]),
            pick_rows(padded[1:2, :-2], partner_rows[:, :, 1]),
            pick_rows(padded[2:3, 1:-1], partner_rows[:, :, 2]),
            pick_rows(padded[0:1, 1:-1], partner_rows[:, :, 3]),
        ],
        axis=2,
    )
    values = received * live_mask[..., None]
    return add_rows(blocks, own_rows, values)


def gram_matrix(left, right, weight):
    local_gram = jnp.einsum(
        "gsir,gsic->rc", left * weight[..., None], right, precision=lax.Precision.HIGHEST
    )
    return lax.psum(local_gram, ("group", "sub"))


def spd_solve(matrix, rhs_block):
    factor = jnp.linalg.cholesky(matrix)
    half = lax.linalg.triangular_solve(factor, rhs_block, left_side=True, lower=True)
    return lax.linalg.triangular_solve(factor, half, left_side=True, lower=True, transpose_a=True)


def contract(blocks, mixing):
    return jnp.einsum("gsir,rc->gsic", blocks, mixing, precision=lax.Precision.HIGHEST)


def shards(
    schur, local_inverse, rhs_parts, basis, coarse_map, coarse_inverse, shared_rows, shared_counts
):
    capacity = shared_rows.shape[-1]
    rows_local = rhs_parts.shape[2]
    columns = rhs_parts.shape[3]
    coarse_total = coarse_inverse.shape[2]
    live_mask = (jnp.arange(capacity, dtype=jnp.int32) < shared_counts[..., None]).astype(
        jnp.float32
    )
    own_rows = shared_rows[:, :, 0]
    partner_rows = shared_rows[:, :, 1]
    weight = 1.0 / count_rows(own_rows, live_mask, rows_local)
    selector = (
        coarse_map.reshape(-1)[:, None] == jnp.arange(coarse_total, dtype=jnp.int32)[None, :]
    ).astype(jnp.float32)
    selector_half = selector.astype(jnp.bfloat16)
    full_inverse = coarse_inverse[0]

    def precondition(resid):
        scaled = (weight[..., None] * resid).astype(jnp.bfloat16)
        local_part = jnp.einsum(
            "gsij,gsjr->gsir", local_inverse, scaled, preferred_element_type=jnp.float32
        )
        coarse_local = jnp.einsum(
            "gsmi,gsir->gsmr", basis, scaled, preferred_element_type=jnp.float32
        )
        contrib = jnp.dot(
            selector.T, coarse_local.reshape(-1, columns), precision=lax.Precision.HIGHEST
        )
        coarse_residual = lax.psum(contrib, "sub")
        coarse_rounded = coarse_residual.astype(jnp.bfloat16)
        row_values = jnp.dot(
            full_inverse, coarse_rounded, preferred_element_type=jnp.float32
        ).astype(jnp.bfloat16)
        coarse_values = lax.all_gather(row_values, "sub", axis=0, tiled=True)
        picked = (
            jnp.dot(selector_half, coarse_values, preferred_element_type=jnp.float32)
            .astype(jnp.bfloat16)
            .reshape(coarse_local.shape)
        )
        coarse_part = jnp.einsum(
            "gsmi,gsmr->gsir", basis, picked, preferred_element_type=jnp.float32
        )
        smoothed = weight[..., None] * (local_part + coarse_part)
        return assemble(smoothed, own_rows, partner_rows, live_mask)

    residual = assemble(rhs_parts.astype(jnp.float32), own_rows, partner_rows, live_mask)
    solution = jnp.zeros_like(residual)
    precond = precondition(residual)
    direction = precond
    inner = gram_matrix(precond, residual, weight)
    for iteration in range(ITERS):
        local_image = jnp.einsum(
            "gsij,gsjr->gsir",
            schur,
            direction.astype(jnp.bfloat16),
            preferred_element_type=jnp.float32,
        )
        image = assemble(local_image, own_rows, partner_rows, live_mask)
        curvature = gram_matrix(direction, image, weight)
        step_size = spd_solve(curvature, inner)
        solution = solution + contract(direction, step_size)
        residual = residual - contract(image, step_size)
        if iteration + 1 < ITERS:
            precond = precondition(residual)
            inner_next = gram_matrix(precond, residual, weight)
            conjugacy = spd_solve(inner, inner_next)
            direction = precond + contract(direction, conjugacy)
            inner = inner_next
    return (solution, residual)


def solution(mesh):
    placed = (
        P("group", "sub", None, None),
        P("group", "sub", None, None),
        P("group", "sub", None, None),
        P("group", "sub", None, None),
        P("group", "sub", None),
        P("group", "sub", None),
        P("group", "sub", None, None, None),
        P("group", "sub", None),
    )
    return jax.shard_map(
        shards,
        mesh=mesh,
        in_specs=placed,
        out_specs=(P("group", "sub", None, None), P("group", "sub", None, None)),
        check_vma=False,
    )
```

profile of v0, /device:TPU:1, one launch (start us, length us, event | category | flops | bytes accessed | tf_op | source)
XLA Modules:
  0.0 1686.3 jit_solution(6008829933205526659)
XLA Ops:
  44.1 14.3 collective-permute-done.3
  78.5 66.6 %all-reduce.19 = bf16[1024,128]{1,0:T(8,128)(2,1)} all-reduce(f32[1024,128]{1,0:T(8,128)S(1)} %fusion.81), channel_id=1, replica_groups=mesh['group'=8,'sub'=16] {'sub'}, use_global_device_ids=true, to_apply=%region_2.0 | all-reduce | flops 131072 | bytes 786432 | tf_op jit(solution)/shard_map/psum | solution.py:106
  146.2 18.0 %all_gather.9 = bf16[1024,128]{1,0:T(8,128)(2,1)} all-gather(bf16[64,128]{1,0:T(8,128)(2,1)S(1)} %fusion.21), channel_id=1, replica_groups=mesh['group'=8,'sub'=16] {'sub'}, dimensions={0}, use_global_device_ids=true | all-gather | bytes 278528 | tf_op jit(solution)/shard_map/all_gather | solution.py:111
  165.8 27.7 %collective-permute-start.4 = (f32[1,1,1024,128]{2,3,1,0:T(8,128)S(1)}, f32[1,1,1024,128]{2,3,1,0:T(8,128)S(1)}, u32[]{:S(2)}, u32[]{:S(2)}) collective-permute-start(f32[1,1,1024,128]{2,3,1,0:T(8,128)S(1)} %bitcast.401), channel_id=1, source_target_pairs={{0,16},{16,32},{32,48},{48,64},{64,80},{80,96},{96,112},{1,17},{17... | collective-permute-start | bytes 1572872 | tf_op jit(solution)/shard_map/ppermute | solution.py:14
  222.3 14.5 collective-permute-done.7
  298.6 15.6 collective-permute-done.11
  335.6 149.4 %all-reduce.18.cloned.1.call-done = (f32[128,128]{0,1:T(8,128)}, f32[128,128]{0,1:T(8,128)}) async-done(((f32[128,128]{0,1:T(8,128)}, f32[128,128]{0,1:T(8,128)}), (f32[128,128]{0,1:T(8,128)}, f32[128,128]{0,1:T(8,128)})) %all-reduce.18.cloned.1.call-update) | async-done | bytes 131088 | tf_op jit(solution)/shard_map/psum | solution.py:63
  488.4 12.5 cholesky.89
  502.3 9.8 custom-call.73
  518.9 64.9 %all-reduce.20 = bf16[1024,128]{1,0:T(8,128)(2,1)} all-reduce(f32[1024,128]{1,0:T(8,128)} %fusion.80), channel_id=1, replica_groups=mesh['group'=8,'sub'=16] {'sub'}, use_global_device_ids=true, to_apply=%region_9.13 | all-reduce | flops 131072 | bytes 786432 | tf_op jit(solution)/shard_map/psum | solution.py:106
  584.9 18.3 %all_gather.10 = bf16[1024,128]{1,0:T(8,128)(2,1)} all-gather(bf16[64,128]{1,0:T(8,128)(2,1)S(1)} %fusion.22), channel_id=1, replica_groups=mesh['group'=8,'sub'=16] {'sub'}, dimensions={0}, use_global_device_ids=true | all-gather | bytes 278528 | tf_op jit(solution)/shard_map/all_gather | solution.py:111
  605.6 21.6 %collective-permute-start.12 = (f32[1,1,1024,128]{2,3,1,0:T(8,128)}, f32[1,1,1024,128]{2,3,1,0:T(8,128)S(1)}, u32[]{:S(2)}, u32[]{:S(2)}) collective-permute-start(f32[1,1,1024,128]{2,3,1,0:T(8,128)} %bitcast.405), channel_id=1, source_target_pairs={{0,16},{16,32},{32,48},{48,64},{64,80},{80,96},{96,112},{1,17},{17... | collective-permute-start | bytes 1572872 | tf_op jit(solution)/shard_map/ppermute | solution.py:14
  647.9 12.5 cholesky.100
  699.7 9.8 custom-call.75
  709.5 135.7 %all-reduce.10.cloned.1.call-done = f32[128,128]{0,1:T(8,128)} async-done(((f32[128,128]{0,1:T(8,128)}), f32[128,128]{0,1:T(8,128)}) %all-reduce.10.cloned.1.call-update) | async-done | bytes 65552 | tf_op jit(solution)/shard_map/psum | solution.py:63
  882.4 13.5 collective-permute-done.19
  911.8 8.3 scatter_custom_fusion.5
  923.4 144.1 %all-reduce.12.cloned.1.call-done = f32[128,128]{0,1:T(8,128)} async-done(((f32[128,128]{0,1:T(8,128)}), f32[128,128]{0,1:T(8,128)}) %all-reduce.12.cloned.1.call-update) | async-done | bytes 65552 | tf_op jit(solution)/shard_map/psum | solution.py:63
  1070.6 13.2 cholesky.111
  1087.4 11.3 custom-call.77
  1107.0 64.4 %all-reduce.21 = bf16[1024,128]{1,0:T(8,128)(2,1)} all-reduce(f32[1024,128]{1,0:T(8,128)} %fusion.79), channel_id=1, replica_groups=mesh['group'=8,'sub'=16] {'sub'}, use_global_device_ids=true, to_apply=%region_14.18 | all-reduce | flops 131072 | bytes 786432 | tf_op jit(solution)/shard_map/psum | solution.py:106
  1172.4 18.2 %all_gather.11 = bf16[1024,128]{1,0:T(8,128)(2,1)} all-gather(bf16[64,128]{1,0:T(8,128)(2,1)S(1)} %fusion.23), channel_id=1, replica_groups=mesh['group'=8,'sub'=16] {'sub'}, dimensions={0}, use_global_device_ids=true | all-gather | bytes 278528 | tf_op jit(solution)/shard_map/all_gather | solution.py:111
  1193.0 21.2 %collective-permute-start.20 = (f32[1,1,1024,128]{2,3,1,0:T(8,128)}, f32[1,1,1024,128]{2,3,1,0:T(8,128)S(1)}, u32[]{:S(2)}, u32[]{:S(2)}) collective-permute-start(f32[1,1,1024,128]{2,3,1,0:T(8,128)} %bitcast.397), channel_id=1, source_target_pairs={{0,16},{16,32},{32,48},{48,64},{64,80},{80,96},{96,112},{1,17},{17... | collective-permute-start | bytes 1572872 | tf_op jit(solution)/shard_map/ppermute | solution.py:14
  1233.2 11.7 cholesky.122
  1274.6 8.2 scatter_custom_fusion.6
  1286.8 9.8 custom-call.79
  1296.6 134.3 %all-reduce.14.cloned.1.call-done = f32[128,128]{1,0:T(8,128)} async-done(((f32[128,128]{1,0:T(8,128)}), f32[128,128]{1,0:T(8,128)}) %all-reduce.14.cloned.1.call-update) | async-done | bytes 65552 | tf_op jit(solution)/shard_map/psum | solution.py:63
  1464.9 16.9 %collective-permute-done.27 = f32[3,1,1024,128]{2,3,1,0:T(8,128)} collective-permute-done((f32[3,1,1024,128]{2,3,1,0:T(8,128)}, f32[3,1,1024,128]{2,3,1,0:T(8,128)}, u32[]{:S(2)}, u32[]{:S(2)}) %collective-permute-start.27) | collective-permute-done | bytes 1572896 | tf_op jit(solution)/shard_map/ppermute | solution.py:14
  1494.4 8.5 scatter_custom_fusion.7
  1508.2 142.1 %all-reduce.16.cloned.1.call-done = f32[128,128]{0,1:T(8,128)} async-done(((f32[128,128]{0,1:T(8,128)}), f32[128,128]{0,1:T(8,128)}) %all-reduce.16.cloned.1.call-update) | async-done | bytes 65552 | tf_op jit(solution)/shard_map/psum | solution.py:63
  1652.2 11.7 cholesky.133
  1665.2 9.8 custom-call.81
  (313 shorter events, 432.7 us)
Async XLA Ops:
  7.2 477.8 %all-reduce.18.cloned.1.call-start = ((), (), s32[]{:S(2)}) async-start(), calls=%async_computation.4 | async-start | bytes 262144 | tf_op jit(solution)/shard_map/psum | solution.py:63
  9.2 10.9 collective-permute-start
  13.7 10.8 collective-permute-start.1
  26.9 31.5 %collective-permute-start.3 = (f32[3,1,1024,128]{3,2,1,0:T(8,128)}, f32[3,1,1024,128]{3,2,1,0:T(8,128)}, u32[]{:S(2)}, u32[]{:S(2)}) collective-permute-start(f32[3,1,1024,128]{3,2,1,0:T(8,128)} %pad_maximum_fusion), channel_id=1, source_target_pairs={{0,1},{1,2},{2,3},{3,4},{4,5},{5,6},{6,7},{7,8},{8,9},{9,10},{10,1... | collective-permute-start | bytes 4718600 | tf_op jit(solution)/shard_map/ppermute | solution.py:14
  31.3 32.4 %collective-permute-start.2 = (f32[3,1,1024,128]{3,2,1,0:T(8,128)}, f32[3,1,1024,128]{3,2,1,0:T(8,128)}, u32[]{:S(2)}, u32[]{:S(2)}) collective-permute-start(f32[3,1,1024,128]{3,2,1,0:T(8,128)} %pad_maximum_fusion), channel_id=1, source_target_pairs={{1,0},{2,1},{3,2},{4,3},{5,4},{6,5},{7,6},{8,7},{9,8},{10,9},{11,1... | collective-permute-start | bytes 4718600 | tf_op jit(solution)/shard_map/ppermute | solution.py:17
  165.8 33.9 %collective-permute-start.4 = (f32[1,1,1024,128]{2,3,1,0:T(8,128)S(1)}, f32[1,1,1024,128]{2,3,1,0:T(8,128)S(1)}, u32[]{:S(2)}, u32[]{:S(2)}) collective-permute-start(f32[1,1,1024,128]{2,3,1,0:T(8,128)S(1)} %bitcast.401), channel_id=1, source_target_pairs={{0,16},{16,32},{32,48},{48,64},{64,80},{80,96},{96,112},{1,17},{17... | collective-permute-start | bytes 1572872 | tf_op jit(solution)/shard_map/ppermute | solution.py:14
  193.6 10.5 collective-permute-start.5
  205.4 31.3 %collective-permute-start.7 = (f32[3,1,1024,128]{2,3,1,0:T(8,128)}, f32[3,1,1024,128]{2,3,1,0:T(8,128)}, u32[]{:S(2)}, u32[]{:S(2)}) collective-permute-start(f32[3,1,1024,128]{2,3,1,0:T(8,128)} %pad_maximum_fusion.1), channel_id=1, source_target_pairs={{0,1},{1,2},{2,3},{3,4},{4,5},{5,6},{6,7},{7,8},{8,9},{9,10},{10,1... | collective-permute-start | bytes 4718600 | tf_op jit(solution)/shard_map/ppermute | solution.py:14
  210.0 33.7 %collective-permute-start.6 = (f32[3,1,1024,128]{2,3,1,0:T(8,128)}, f32[3,1,1024,128]{2,3,1,0:T(8,128)}, u32[]{:S(2)}, u32[]{:S(2)}) collective-permute-start(f32[3,1,1024,128]{2,3,1,0:T(8,128)} %pad_maximum_fusion.1), channel_id=1, source_target_pairs={{1,0},{2,1},{3,2},{4,3},{5,4},{6,5},{7,6},{8,7},{9,8},{10,9},{11,1... | collective-permute-start | bytes 4718600 | tf_op jit(solution)/shard_map/ppermute | solution.py:17
  261.9 14.2 collective-permute-start.8
  269.9 10.5 collective-permute-start.9
  281.8 32.4 %collective-permute-start.11 = (f32[3,1,1024,128]{2,3,1,0:T(8,128)}, f32[3,1,1024,128]{2,3,1,0:T(8,128)}, u32[]{:S(2)}, u32[]{:S(2)}) collective-permute-start(f32[3,1,1024,128]{2,3,1,0:T(8,128)} %pad_maximum_fusion.2), channel_id=1, source_target_pairs={{0,1},{1,2},{2,3},{3,4},{4,5},{5,6},{6,7},{7,8},{8,9},{9,10},{10,1... | collective-permute-start | bytes 4718600 | tf_op jit(solution)/shard_map/ppermute | solution.py:14
  287.5 32.0 %collective-permute-start.10 = (f32[3,1,1024,128]{2,3,1,0:T(8,128)}, f32[3,1,1024,128]{2,3,1,0:T(8,128)}, u32[]{:S(2)}, u32[]{:S(2)}) collective-permute-start(f32[3,1,1024,128]{2,3,1,0:T(8,128)} %pad_maximum_fusion.2), channel_id=1, source_target_pairs={{1,0},{2,1},{3,2},{4,3},{5,4},{6,5},{7,6},{8,7},{9,8},{10,9},{11,1... | collective-permute-start | bytes 4718600 | tf_op jit(solution)/shard_map/ppermute | solution.py:17
  335.5 509.6 %all-reduce.10.cloned.1.call-start = ((), (), s32[]{:S(2)}) async-start(), calls=%async_computation | async-start | bytes 131072 | tf_op jit(solution)/shard_map/psum | solution.py:63
  605.6 28.0 %collective-permute-start.12 = (f32[1,1,1024,128]{2,3,1,0:T(8,128)}, f32[1,1,1024,128]{2,3,1,0:T(8,128)S(1)}, u32[]{:S(2)}, u32[]{:S(2)}) collective-permute-start(f32[1,1,1024,128]{2,3,1,0:T(8,128)} %bitcast.405), channel_id=1, source_target_pairs={{0,16},{16,32},{32,48},{48,64},{64,80},{80,96},{96,112},{1,17},{17... | collective-permute-start | bytes 1572872 | tf_op jit(solution)/shard_map/ppermute | solution.py:14
  627.1 10.7 collective-permute-start.13
  640.4 31.3 %collective-permute-start.15 = (f32[3,1,1024,128]{2,3,1,0:T(8,128)}, f32[3,1,1024,128]{2,3,1,0:T(8,128)}, u32[]{:S(2)}, u32[]{:S(2)}) collective-permute-start(f32[3,1,1024,128]{2,3,1,0:T(8,128)} %pad_maximum_fusion.3), channel_id=1, source_target_pairs={{0,1},{1,2},{2,3},{3,4},{4,5},{5,6},{6,7},{7,8},{8,9},{9,10},{10,1... | collective-permute-start | bytes 4718600 | tf_op jit(solution)/shard_map/ppermute | solution.py:14
  644.6 34.0 %collective-permute-start.14 = (f32[3,1,1024,128]{2,3,1,0:T(8,128)}, f32[3,1,1024,128]{2,3,1,0:T(8,128)}, u32[]{:S(2)}, u32[]{:S(2)}) collective-permute-start(f32[3,1,1024,128]{2,3,1,0:T(8,128)} %pad_maximum_fusion.3), channel_id=1, source_target_pairs={{1,0},{2,1},{3,2},{4,3},{5,4},{6,5},{7,6},{8,7},{9,8},{10,9},{11,1... | collective-permute-start | bytes 4718600 | tf_op jit(solution)/shard_map/ppermute | solution.py:17
  698.7 368.8 %all-reduce.12.cloned.1.call-start = ((), (), s32[]{:S(2)}) async-start(), calls=%async_computation.1 | async-start | bytes 131072 | tf_op jit(solution)/shard_map/psum | solution.py:63
  850.5 8.5 collective-permute-start.16
  853.0 10.5 collective-permute-start.17
  864.8 31.1 %collective-permute-start.19 = (f32[3,1,1024,128]{2,3,1,0:T(8,128)}, f32[3,1,1024,128]{2,3,1,0:T(8,128)}, u32[]{:S(2)}, u32[]{:S(2)}) collective-permute-start(f32[3,1,1024,128]{2,3,1,0:T(8,128)} %pad_maximum_fusion.4), channel_id=1, source_target_pairs={{0,1},{1,2},{2,3},{3,4},{4,5},{5,6},{6,7},{7,8},{8,9},{9,10},{10,1... | collective-permute-start | bytes 4718600 | tf_op jit(solution)/shard_map/ppermute | solution.py:14
  868.9 33.9 %collective-permute-start.18 = (f32[3,1,1024,128]{2,3,1,0:T(8,128)}, f32[3,1,1024,128]{2,3,1,0:T(8,128)}, u32[]{:S(2)}, u32[]{:S(2)}) collective-permute-start(f32[3,1,1024,128]{2,3,1,0:T(8,128)} %pad_maximum_fusion.4), channel_id=1, source_target_pairs={{1,0},{2,1},{3,2},{4,3},{5,4},{6,5},{7,6},{8,7},{9,8},{10,9},{11,1... | collective-permute-start | bytes 4718600 | tf_op jit(solution)/shard_map/ppermute | solution.py:17
  922.9 507.9 %all-reduce.14.cloned.1.call-start = ((), (), s32[]{:S(2)}) async-start(), calls=%async_computation.2 | async-start | bytes 131072 | tf_op jit(solution)/shard_map/psum | solution.py:63
  1193.0 27.6 %collective-permute-start.20 = (f32[1,1,1024,128]{2,3,1,0:T(8,128)}, f32[1,1,1024,128]{2,3,1,0:T(8,128)S(1)}, u32[]{:S(2)}, u32[]{:S(2)}) collective-permute-start(f32[1,1,1024,128]{2,3,1,0:T(8,128)} %bitcast.397), channel_id=1, source_target_pairs={{0,16},{16,32},{32,48},{48,64},{64,80},{80,96},{96,112},{1,17},{17... | collective-permute-start | bytes 1572872 | tf_op jit(solution)/shard_map/ppermute | solution.py:14
  1214.2 10.7 collective-permute-start.21
  1227.4 31.3 %collective-permute-start.23 = (f32[3,1,1024,128]{2,3,1,0:T(8,128)}, f32[3,1,1024,128]{2,3,1,0:T(8,128)}, u32[]{:S(2)}, u32[]{:S(2)}) collective-permute-start(f32[3,1,1024,128]{2,3,1,0:T(8,128)} %pad_maximum_fusion.5), channel_id=1, source_target_pairs={{0,1},{1,2},{2,3},{3,4},{4,5},{5,6},{6,7},{7,8},{8,9},{9,10},{10,1... | collective-permute-start | bytes 4718600 | tf_op jit(solution)/shard_map/ppermute | solution.py:14
  1231.6 34.0 %collective-permute-start.22 = (f32[3,1,1024,128]{2,3,1,0:T(8,128)}, f32[3,1,1024,128]{2,3,1,0:T(8,128)}, u32[]{:S(2)}, u32[]{:S(2)}) collective-permute-start(f32[3,1,1024,128]{2,3,1,0:T(8,128)} %pad_maximum_fusion.5), channel_id=1, source_target_pairs={{1,0},{2,1},{3,2},{4,3},{5,4},{6,5},{7,6},{8,7},{9,8},{10,9},{11,1... | collective-permute-start | bytes 4718600 | tf_op jit(solution)/shard_map/ppermute | solution.py:17
  1285.8 364.5 %all-reduce.16.cloned.1.call-start = ((), (), s32[]{:S(2)}) async-start(), calls=%async_computation.3 | async-start | bytes 131072 | tf_op jit(solution)/shard_map/psum | solution.py:63
  1438.9 10.5 collective-permute-start.25
  1450.7 31.1 %collective-permute-start.27 = (f32[3,1,1024,128]{2,3,1,0:T(8,128)}, f32[3,1,1024,128]{2,3,1,0:T(8,128)}, u32[]{:S(2)}, u32[]{:S(2)}) collective-permute-start(f32[3,1,1024,128]{2,3,1,0:T(8,128)} %pad_maximum_fusion.6), channel_id=1, source_target_pairs={{0,1},{1,2},{2,3},{3,4},{4,5},{5,6},{6,7},{7,8},{8,9},{9,10},{10,1... | collective-permute-start | bytes 4718600 | tf_op jit(solution)/shard_map/ppermute | solution.py:14
  1454.9 32.2 %collective-permute-start.26 = (f32[3,1,1024,128]{2,3,1,0:T(8,128)}, f32[3,1,1024,128]{2,3,1,0:T(8,128)}, u32[]{:S(2)}, u32[]{:S(2)}) collective-permute-start(f32[3,1,1024,128]{2,3,1,0:T(8,128)} %pad_maximum_fusion.6), channel_id=1, source_target_pairs={{1,0},{2,1},{3,2},{4,3},{5,4},{6,5},{7,6},{8,7},{9,8},{10,9},{11,1... | collective-permute-start | bytes 4718600 | tf_op jit(solution)/shard_map/ppermute | solution.py:17
  (35 other events, 1593.9 us)
Sparse Core Ops, SparseCore 0:
  335.7 149.2 all-reduce.17
  698.8 146.2 all-reduce.9
  923.1 144.4 all-reduce.11
  1286.0 144.8 all-reduce.13
  1505.9 144.4 all-reduce.15
where the time goes:
time: 1700 us; the launch traced here: 1690 us
  waiting for transfers between devices  842 us (50%)
  blocking collectives  250 us (15%)
  other arithmetic  218 us (13%)
  local copies, waits for them, and re-layouts  155 us (9%)
  starting transfers between devices  143 us (8%)
  matrix products  63.4 us (4%)
    psum x5, waiting for transfers between devices, gram_matrix(): return lax.psum(local_gram, ('group', 'sub'))  706 us
    psum x3, blocking collectives, precondition(): coarse_residual = lax.psum(contrib, 'sub')  196 us
    ppermute x14, starting transfers between devices, extended(): lax.ppermute(lax.slice_in_dim(block, block.shape[dim] - width, None, axis...  119 us
    ppermute x14, waiting for transfers between devices, extended(): lax.ppermute(lax.slice_in_dim(block, block.shape[dim] - width, None, axis...  103 us
    gather x28, local copies, waits for them, and re-layouts, pick_rows(): source_block[rows_at]  70.6 us
    another operation x15, other arithmetic, spd_solve(): factor = jnp.linalg.cholesky(matrix)  66 us
    another operation x10, other arithmetic, spd_solve(): lax.linalg.triangular_solve(factor, half, left_side=True, lower=True, tra...  55.3 us
    all_gather x3, blocking collectives, precondition(): coarse_values = lax.all_gather(row_values, 'sub', axis=0, tiled=True)  54.4 us
  transfers between devices with their start and end apart: 33, of which 27 were waited for; matrix products, arithmetic and copies ran while one was open for 10% of the time, Pallas kernels for 0%

commit v1 on v0

v1 whole, which is shorter than its diff:
```python
import functools

import jax
import jax.numpy as jnp
from jax import lax
from jax.experimental import pallas as pl
from jax.experimental.pallas import tpu as pltpu
from jax.sharding import PartitionSpec as P

BF = jnp.bfloat16
F32 = jnp.float32
MESH = pl.DeviceIdType.MESH
N_GROUP = 8
N_SUB = 16
NL = 1024
ZONE = 256
NR = 128
NC = 32
NC_ALL = NC * N_SUB
OWN_ROWS = 64
AR_ROWS = (256, 256, 128, 128)


def split(x):
    hi = x.astype(BF)
    lo = (x - hi.astype(F32)).astype(BF)
    return jnp.concatenate([hi, lo], axis=-1)


def fold(y):
    return y[:, :NR] + y[:, NR:]


def dot(a, b, dims=((1,), (0,))):
    return lax.dot_general(a, b, (dims, ((), ())), preferred_element_type=F32)


def small(a, b):
    return jnp.dot(a, b, precision=lax.Precision.HIGHEST, preferred_element_type=F32)


def gram(left, right):
    full = dot(left, right, ((0,), (0,)))
    half = full[:NR] + full[NR:]
    return half[:, :NR] + half[:, NR:]


def sym(a):
    return 0.5 * (a + a.T)


def combine(blocks, mixing):
    halves = split(mixing)
    return fold(dot(blocks, jnp.concatenate([halves, halves], axis=0)))


def invert_steps(mat, first, last):
    lane = lax.broadcasted_iota(jnp.int32, (NR, NR), 1)
    lane_row = lax.broadcasted_iota(jnp.int32, (1, NR), 1)
    sub = lax.broadcasted_iota(jnp.int32, (NR, NR), 0)

    def step(k, carry):
        a = mat[...]
        row = mat[pl.ds(k, 1), :]
        here = lane == k
        col = jnp.sum(jnp.where(here, a, 0.0), axis=1, keepdims=True)
        pivot = jnp.sum(jnp.where(lane_row == k, row, 0.0), axis=1, keepdims=True)
        scaled = jnp.where(lane_row == k, 1.0, row) / pivot
        new = jnp.where(here, 0.0, a) - col * scaled
        mat[...] = jnp.where(sub == k, scaled, new)
        return carry

    lax.fori_loop(first, last, step, 0)


def kernel(
    schur_h, linv_h, rhs, basis, cmap, cinv, rows, counts,
    x_out, r_out,
    schur, linv, perm, weight, mult, sent, got0, got, r0, xw, xz, loc, base,
    cl_mine, cl_all, map_mine, map_all, e_mine, e_all, coarse, mu, inv,
    ar_in, ar_r1, ar_p, ar_r2, ar_q, ar_out,
    load_sem, xs, xr, cs, cr, ms, mr, es, er, as1, ar1, as2, ar2, as3, ar3,
):
    g = lax.axis_index("group")
    s = lax.axis_index("sub")
    started = []

    def remote(src, dst, send_sem, recv_sem, target):
        copy = pltpu.make_async_remote_copy(
            src_ref=src, dst_ref=dst, send_sem=send_sem, recv_sem=recv_sem,
            device_id=target, device_id_type=MESH,
        )
        copy.start()
        started.append(copy)
        return copy

    load_l = pltpu.make_async_copy(linv_h, linv, load_sem.at[0])
    load_s = pltpu.make_async_copy(schur_h, schur, load_sem.at[1])
    load_l.start()
    load_s.start()

    barrier = pltpu.get_barrier_semaphore()
    mates = [(g, lax.rem(s + k, N_SUB)) for k in range(1, N_SUB)]
    peers = [(lax.rem(g + k, N_GROUP), s) for k in range(1, N_GROUP)]
    for target in mates + peers:
        pl.semaphore_signal(barrier, inc=1, device_id=target, device_id_type=MESH)

    map_mine[...] = jnp.zeros((8, NR), jnp.int32)
    map_mine[0:1, 0:NC] = cmap[...]
    tile = jnp.broadcast_to(map_mine[0:1, :], (8, NR))
    tile = pltpu.roll(tile, NC * lax.rem(s, 4), 1)
    at_row = lax.broadcasted_iota(jnp.int32, (8, NR), 0) == lax.div(s, 4)
    map_mine[...] = jnp.where(at_row, tile, 0)

    pl.semaphore_wait(barrier, len(mates) + len(peers))

    around = [
        (g, lax.rem(s + 1, N_SUB)),
        (g, lax.rem(s + N_SUB - 1, N_SUB)),
        (lax.rem(g + 1, N_GROUP), s),
        (lax.rem(g + N_GROUP - 1, N_GROUP), s),
    ]

    def send_zone(e, d, src, dst):
        return remote(src, dst.at[d ^ 1], xs.at[e, d], xr.at[e, d ^ 1], around[d])

    def zone(d):
        return pl.ds(ZONE * d, ZONE)

    copies0 = [send_zone(0, d, rhs.at[zone(d)], got0) for d in range(4)]
    map_copies = [
        remote(map_mine, map_all.at[k], ms.at[k], mr.at[k], mates[k - 1])
        for k in range(1, N_SUB)
    ]

    lane = lax.broadcasted_iota(jnp.int32, (1, ZONE), 1)
    at = lax.broadcasted_iota(jnp.int32, (ZONE, ZONE), 0)
    for d in range(4):
        mine = jnp.where(lane < counts[0, d], rows[0, d : d + 1, :] - ZONE * d, -1)
        theirs = rows[1, d : d + 1, :] - ZONE * (d ^ 1)
        place = jnp.where(at == mine, 1.0, 0.0)
        times = 1.0 + jnp.sum(place, axis=1, keepdims=True)
        mult[zone(d), :] = jnp.broadcast_to(times, (ZONE, NR))
        weight[zone(d), :] = jnp.broadcast_to(1.0 / times, (ZONE, NR))
        pick = jnp.where(at == theirs, 1.0, 0.0).astype(BF)
        perm[d] = dot(place.astype(BF), pick, ((1,), (1,))).astype(BF)

    for d in range(4):
        copies0[d ^ 1].wait_recv()
        block = rhs[zone(d), :].astype(F32) + dot(perm[d], got0[d])
        r0[zone(d), :] = block
        xw[0, zone(d), :] = split(weight[zone(d), :] * block)

    def coarse_send(k):
        local = fold(dot(basis[...], xw[k]))
        cl_mine[k] = local
        copies = [
            remote(cl_mine.at[k], cl_all.at[k, s], cs.at[k, i + 1], cr.at[k, i + 1], mates[i])
            for i in range(N_SUB - 1)
        ]
        cl_all[k, s] = local
        return copies

    def coarse_setup():
        for copy in map_copies:
            copy.wait_recv()
        total = map_mine[...]
        for k in range(1, N_SUB):
            total = total + map_all[k]
        at_all = lax.broadcasted_iota(jnp.int32, (NL, NR), 0)
        at_own = lax.broadcasted_iota(jnp.int32, (OWN_ROWS, NR), 0) + OWN_ROWS * s
        hot = jnp.concatenate(
            [jnp.where(at_all == total[i : i + 1, :], 1.0, 0.0).astype(BF) for i in range(4)], axis=1
        )
        hot_own = jnp.concatenate(
            [jnp.where(at_own == total[i : i + 1, :], 1.0, 0.0).astype(BF) for i in range(4)], axis=1
        )
        columns = dot(cinv[...], hot).astype(BF)
        entries = dot(hot_own, columns, ((0,), (0,))).astype(BF)
        e_mine[...] = entries.reshape(N_SUB, NC, NC_ALL)
        copies = [
            remote(
                e_mine.at[lax.rem(s + k, N_SUB)], e_all.at[s], es.at[k], er.at[k], mates[k - 1]
            )
            for k in range(1, N_SUB)
        ]
        e_all[s] = e_mine[s]
        return copies

    def local_apply(matrix, blocks, d):
        return fold(dot(matrix[zone(d), :], blocks))

    def precondition(k, e, during):
        copies = coarse_send(k)
        if k == 0:
            e_copies = coarse_setup()
            load_l.wait()
        blocks = xw[k]
        for d in range(4):
            loc[zone(d), :] = local_apply(linv, blocks, d)
        during()
        if k == 0:
            for copy in e_copies:
                copy.wait_recv()
            total = e_all[0].astype(F32)
            for i in range(1, N_SUB):
                total = total + e_all[i].astype(F32)
            coarse[...] = total.astype(BF)
        for copy in copies:
            copy.wait_recv()
        terms = split(cl_all[k].reshape(NC_ALL, NR))
        picked = split(fold(dot(coarse[...], terms)))
        sends = []
        for d in range(4):
            part = fold(dot(basis[:, zone(d)], picked, ((0,), (0,))))
            sent[e - 1, zone(d), :] = weight[zone(d), :] * (loc[zone(d), :] + part)
            sends.append(send_zone(e, d, sent.at[e - 1, zone(d)], got.at[e - 1]))
        return sends

    def operate(k, e):
        sends = []
        blocks = xz[k]
        for d in range(4):
            sent[e - 1, zone(d), :] = local_apply(schur, blocks, d)
            sends.append(send_zone(e, d, sent.at[e - 1, zone(d)], got.at[e - 1]))
        return sends

    def assembled(e, sends, d):
        sends[d ^ 1].wait_recv()
        return sent[e - 1, zone(d), :] + fold(dot(perm[d], split(got[e - 1, d])))

    def finish_z(k, e, sends):
        for d in range(4):
            xz[k, zone(d), :] = split(assembled(e, sends, d))

    def finish_q(k, e, sends):
        for d in range(4):
            xw[k + 1, zone(d), :] = split(weight[zone(d), :] * assembled(e, sends, d))

    def reduce_start(i):
        share = AR_ROWS[i] // N_GROUP
        copies = []
        for k in range(1, N_GROUP):
            src = ar_in[i].at[pl.ds(pl.multiple_of(share * peers[k - 1][0], 8), share)]
            copies.append(
                remote(src, ar_r1[i].at[g], as1.at[i, k], ar1.at[i, k], peers[k - 1])
            )
        ar_r1[i][g] = ar_in[i][pl.ds(pl.multiple_of(share * g, 8), share), :]
        return copies

    def reduce_middle(i, waits):
        for copy in waits:
            copy.wait_recv()
        total = ar_r1[i][0]
        for k in range(1, N_GROUP):
            total = total + ar_r1[i][k]
        ar_p[i][...] = total
        copies = [
            remote(ar_p[i], ar_r2[i].at[s], as2.at[i, k], ar2.at[i, k], mates[k - 1])
            for k in range(1, N_SUB)
        ]
        ar_r2[i][s] = total
        return copies

    def reduce_last(i, waits):
        share = AR_ROWS[i] // N_GROUP
        for copy in waits:
            copy.wait_recv()
        total = ar_r2[i][0]
        for k in range(1, N_SUB):
            total = total + ar_r2[i][k]
        ar_q[i][...] = total
        mine = pl.ds(pl.multiple_of(share * g, 8), share)
        copies = [
            remote(ar_q[i], ar_out[i].at[mine], as3.at[i, k], ar3.at[i, k], peers[k - 1])
            for k in range(1, N_GROUP)
        ]
        ar_out[i][mine, :] = total
        return copies

    def reduce_wait(waits):
        for copy in waits:
            copy.wait_recv()

    def nothing():
        pass

    state = {}

    sends = precondition(0, 1, nothing)
    finish_z(0, 1, sends)
    load_s.wait()
    sends = operate(0, 2)
    ar_in[0][0:NR, :] = gram(xz[0], xw[0])
    finish_q(0, 2, sends)
    ar_in[0][NR:, :] = gram(xz[0], xw[1])
    state["a"] = reduce_start(0)

    def during1():
        state["a"] = reduce_middle(0, state["a"])

    sends = precondition(1, 3, during1)
    state["a"] = reduce_last(0, state["a"])
    finish_z(1, 3, sends)
    sends = operate(1, 4)
    ar_in[1][0:NR, :] = gram(xz[1], xw[1])
    reduce_wait(state["a"])
    mu[0] = ar_out[0][0:NR, :]
    inv[0] = sym(ar_out[0][NR:, :])
    invert_steps(inv.at[0], 0, 32)
    finish_q(1, 4, sends)
    ar_in[1][NR:, :] = gram(xz[1], xw[2])
    state["b"] = reduce_start(1)

    def during2():
        invert_steps(inv.at[0], 32, 64)
        state["b"] = reduce_middle(1, state["b"])

    sends = precondition(2, 5, during2)
    invert_steps(inv.at[0], 64, 96)
    state["b"] = reduce_last(1, state["b"])
    finish_z(2, 5, sends)
    sends = operate(2, 6)
    ar_in[2][...] = gram(xz[2], xw[2])
    state["c"] = reduce_start(2)
    invert_steps(inv.at[0], 96, 128)
    reduce_wait(state["b"])
    finish_q(2, 6, sends)
    ar_in[3][...] = gram(xz[2], xw[3])
    state["d"] = reduce_start(3)
    state["c"] = reduce_middle(2, state["c"])
    m0 = mu[0]
    m2 = sym(ar_out[1][0:NR, :])
    m3 = sym(ar_out[1][NR:, :])
    inv1 = inv[0]
    t0 = small(inv1, m0)
    t2 = small(inv1, m2)
    t3 = small(inv1, m3)
    inv[1] = sym(m3 - small(m2, t2))
    h1 = sym(ar_out[0][NR:, :]) - small(m2, t0)
    state["d"] = reduce_middle(3, state["d"])
    state["c"] = reduce_last(2, state["c"])
    invert_steps(inv.at[1], 0, 64)
    state["d"] = reduce_last(3, state["d"])
    invert_steps(inv.at[1], 64, 128)
    reduce_wait(state["c"])
    m4 = sym(ar_out[2][...])
    inv2 = inv[1]
    s23 = m4 - small(m2, t3)
    y = small(inv2, s23)
    u1 = small(inv2, h1)
    h2 = m2 - small(m3, t0) - lax.dot_general(
        s23, u1, (((0,), (0,)), ((), ())), precision=lax.Precision.HIGHEST, preferred_element_type=F32
    )
    part = small(m3, t3) + lax.dot_general(
        s23, y, (((0,), (0,)), ((), ())), precision=lax.Precision.HIGHEST, preferred_element_type=F32
    )
    a0 = t0 - small(t2, u1)
    d0 = small(t2, y) - t3
    x_out[...] = combine(xz[0], a0) + combine(xz[1], u1)
    xd = xz[2]
    base[0] = split(
        xd[:, :NR].astype(F32) + xd[:, NR:].astype(F32) - combine(xz[1], y) + combine(xz[0], d0)
    )
    r_out[...] = r0[...] - mult[...] * (combine(xw[1], a0) + combine(xw[2], u1))
    qd = xw[3]
    base[1] = split(
        qd[:, :NR].astype(F32) + qd[:, NR:].astype(F32) - combine(xw[2], y) + combine(xw[1], d0)
    )
    reduce_wait(state["d"])
    inv[2] = sym(ar_out[3][...] - part)
    invert_steps(inv.at[2], 0, 128)
    c2 = small(inv[2], h2)
    x_out[...] = x_out[...] + combine(base[0], c2)
    r_out[...] = r_out[...] - mult[...] * combine(base[1], c2)
    for copy in started:
        copy.wait_send()


def shards(
    schur, local_inverse, rhs_parts, basis, coarse_map, coarse_inverse, shared_rows, shared_counts
):
    vmem = pl.BlockSpec(memory_space=pltpu.VMEM)
    anywhere = pl.BlockSpec(memory_space=pl.ANY)
    dma = pltpu.SemaphoreType.DMA
    ar_shapes = [r // N_GROUP for r in AR_ROWS]
    scratch = [
        pltpu.VMEM((NL, NL), BF),
        pltpu.VMEM((NL, NL), BF),
        pltpu.VMEM((4, ZONE, ZONE), BF),
        pltpu.VMEM((NL, NR), F32),
        pltpu.VMEM((NL, NR), F32),
        pltpu.VMEM((6, NL, NR), F32),
        pltpu.VMEM((4, ZONE, NR), BF),
        pltpu.VMEM((6, 4, ZONE, NR), F32),
        pltpu.VMEM((NL, NR), F32),
        pltpu.VMEM((4, NL, 2 * NR), BF),
        pltpu.VMEM((3, NL, 2 * NR), BF),
        pltpu.VMEM((NL, NR), F32),
        pltpu.VMEM((2, NL, 2 * NR), BF),
        pltpu.VMEM((3, NC, NR), F32),
        pltpu.VMEM((3, N_SUB, NC, NR), F32),
        pltpu.VMEM((8, NR), jnp.int32),
        pltpu.VMEM((N_SUB, 8, NR), jnp.int32),
        pltpu.VMEM((N_SUB, NC, NC_ALL), BF),
        pltpu.VMEM((N_SUB, NC, NC_ALL), BF),
        pltpu.VMEM((NC, NC_ALL), BF),
        pltpu.VMEM((1, NR, NR), F32),
        pltpu.VMEM((3, NR, NR), F32),
        [pltpu.VMEM((r, NR), F32) for r in AR_ROWS],
        [pltpu.VMEM((N_GROUP, r, NR), F32) for r in ar_shapes],
        [pltpu.VMEM((r, NR), F32) for r in ar_shapes],
        [pltpu.VMEM((N_SUB, r, NR), F32) for r in ar_shapes],
        [pltpu.VMEM((r, NR), F32) for r in ar_shapes],
        [pltpu.VMEM((r, NR), F32) for r in AR_ROWS],
        dma((2,)),
        dma((7, 4)),
        dma((7, 4)),
        dma((3, N_SUB)),
        dma((3, N_SUB)),
        dma((N_SUB,)),
        dma((N_SUB,)),
        dma((N_SUB,)),
        dma((N_SUB,)),
        dma((4, N_GROUP)),
        dma((4, N_GROUP)),
        dma((4, N_SUB)),
        dma((4, N_SUB)),
        dma((4, N_GROUP)),
        dma((4, N_GROUP)),
    ]
    out = jax.ShapeDtypeStruct((NL, NR), F32)
    x, r = pl.pallas_call(
        kernel,
        out_shape=(out, out),
        in_specs=[anywhere, anywhere, vmem, vmem, vmem, vmem, vmem,
                  pl.BlockSpec(memory_space=pltpu.SMEM)],
        out_specs=(vmem, vmem),
        scratch_shapes=scratch,
        compiler_params=pltpu.CompilerParams(
            collective_id=0, has_side_effects=True, vmem_limit_bytes=48 * 1024 * 1024
        ),
        name="block_cg",
    )(
        schur[0, 0], local_inverse[0, 0], rhs_parts[0, 0], basis[0, 0], coarse_map[0],
        coarse_inverse[0], shared_rows[0, 0], shared_counts[0],
    )
    return x[None, None], r[None, None]


def solution(mesh):
    placed = (
        P("group", "sub", None, None),
        P("group", "sub", None, None),
        P("group", "sub", None, None),
        P("group", "sub", None, None),
        P("group", "sub", None),
        P("group", "sub", None),
        P("group", "sub", None, None, None),
        P("group", "sub", None),
    )
    return jax.shard_map(
        shards,
        mesh=mesh,
        in_specs=placed,
        out_specs=(P("group", "sub", None, None), P("group", "sub", None, None)),
        check_vma=False,
    )
```

time: 1700 us -> 129 us (0.08)
  waiting for transfers between devices: 842 us -> 0 us
  blocking collectives: 250 us -> 0 us
  other arithmetic: 218 us -> 0 us
  local copies, waits for them, and re-layouts: 155 us -> 9.46 us
  starting transfers between devices: 143 us -> 0 us
  Pallas kernels: 0 us -> 118 us
  matrix products: 63.4 us -> 0 us
    psum x5 -> x0, waiting for transfers between devices: 706 us -> none  [gram_matrix(): return lax.psum(local_gram, ('group', 'sub'))]
    psum x3 -> x0, blocking collectives: 196 us -> none  [precondition(): coarse_residual = lax.psum(contrib, 'sub')]
    another operation x37 -> x0, other arithmetic: 166 us -> none  [the longest x15 66 us: spd_solve(): factor = jnp.linalg.cholesky(matrix)]
    ppermute x28 -> x0, starting transfers between devices: 142 us -> none  [the longest x14 119 us: extended(): lax.ppermute(lax.slice_in_dim(block, block.shape[dim] - width, None, axis...]
    ppermute x28 -> x0, waiting for transfers between devices: 136 us -> none  [the longest x14 103 us: extended(): lax.ppermute(lax.slice_in_dim(block, block.shape[dim] - width, None, axis...]
    pallas_call x0 -> x1, Pallas kernels: none -> 118 us  [shards(): pl.pallas_call(kernel, out_shape=(out, out), in_specs=[anywhere, anywhere...]
    gather x28 -> x0, local copies, waits for them, and re-layouts: 70.6 us -> none  [pick_rows(): source_block[rows_at]]
    dot_general x32 -> x0, matrix products: 56.7 us -> none  [the longest x6 15.1 us: gram_matrix(): jnp.einsum('gsir,gsic->rc', left * weight[..., None], right, precision=la...]
  transfers between devices with their start and end apart: 33 -> 0, of which waited for: 27 -> 0; matrix products, arithmetic and copies ran while one was open for 10% -> 0% of each run, Pallas kernels for 0% -> 0%
where the time goes in v1:
time: 129 us; the launch traced here: 128 us
  Pallas kernels  118 us (91%)
  local copies, waits for them, and re-layouts  9.46 us (7%)
    pallas_call x1, Pallas kernels, shards(): pl.pallas_call(kernel, out_shape=(out, out), in_specs=[anywhere, anywhere...  118 us
    unnamed x18, local copies, waits for them, and re-layouts  9.46 us

profile of v1, /device:TPU:1, one launch (start us, length us, event | category | flops | bytes accessed | tf_op | source)
XLA Modules:
  0.0 127.8 jit_solution(7456801133036006993)
XLA Ops:
  0.6 0.0 copy-start
  0.6 1.6 %copy-done = bf16[1,1,1024,1024]{3,2,1,0:T(8,128)(2,1)S(1)} copy-done((bf16[1,1,1024,1024]{3,2,1,0:T(8,128)(2,1)S(1)}, bf16[1,1,1024,1024]{3,2,1,0:T(8,128)(2,1)}, u32[]{:S(2)}) %copy-start) | copy-done | bytes 2097176
  2.2 0.0 copy-start.1
  2.2 1.6 %copy-done.1 = bf16[1,1,1024,1024]{3,2,1,0:T(8,128)(2,1)S(1)} copy-done((bf16[1,1,1024,1024]{3,2,1,0:T(8,128)(2,1)S(1)}, bf16[1,1,1024,1024]{3,2,1,0:T(8,128)(2,1)}, u32[]{:S(2)}) %copy-start.1) | copy-done | bytes 2097176
  3.8 0.0 copy-start.2
  3.8 0.9 copy-done.2
  4.8 0.0 copy-start.3
  4.8 0.9 copy-done.3
  5.7 0.0 copy-start.4
  5.7 0.8 copy-done.4
  6.5 0.0 copy-start.5
  6.5 0.7 copy-done.5
  7.2 0.0 copy-start.6
  7.2 0.7 copy-done.6
  7.9 0.0 copy-start.7
  7.9 0.7 copy-done.7
  8.5 117.7 %block_cg.1 = (f32[1024,128]{1,0:T(8,128)S(1)}, f32[1024,128]{1,0:T(8,128)S(1)}) custom-call(bf16[1024,1024]{1,0:T(8,128)(2,1)S(1)} %bitcast.10, bf16[1024,1024]{1,0:T(8,128)(2,1)S(1)} %bitcast.11, bf16[1024,128]{1,0:T(8,128)(2,1)S(1)} %bitcast.14, bf16[32,1024]{1,0:T(8,128)(2,1)S(1)} %bitcast.16, s32[1,32]{1,0:T(1,128)S(1)} %bitcast.18, ...), custom_call_target="tpu_custom_call" | custom-call | tf_op jit(solution)/shard_map/block_cg/pallas_call | solution.py:433
  126.2 0.8 copy.12
  127.0 0.8 copy.13
Async XLA Ops:
  0.6 1.6 %copy-start = (bf16[1,1,1024,1024]{3,2,1,0:T(8,128)(2,1)S(1)}, bf16[1,1,1024,1024]{3,2,1,0:T(8,128)(2,1)}, u32[]{:S(2)}) copy-start(bf16[1,1,1024,1024]{3,2,1,0:T(8,128)(2,1)} %param.8) | copy-start | bytes 6291460
  2.2 1.6 %copy-start.1 = (bf16[1,1,1024,1024]{3,2,1,0:T(8,128)(2,1)S(1)}, bf16[1,1,1024,1024]{3,2,1,0:T(8,128)(2,1)}, u32[]{:S(2)}) copy-start(bf16[1,1,1024,1024]{3,2,1,0:T(8,128)(2,1)} %param.9) | copy-start | bytes 6291460
  3.8 0.9 copy-start.2
  4.8 0.9 copy-start.3
  5.7 0.8 copy-start.4
  6.5 0.7 copy-start.5
  7.2 0.7 copy-start.6
  7.9 0.7 copy-start.7

commit v2 on v1

--- a/solution.py
+++ b/solution.py
@@ -56,30 +56,58 @@
 
 def invert_steps(mat, first, last):
     lane = lax.broadcasted_iota(jnp.int32, (NR, NR), 1)
-    lane_row = lax.broadcasted_iota(jnp.int32, (1, NR), 1)
     sub = lax.broadcasted_iota(jnp.int32, (NR, NR), 0)
-
-    def step(k, carry):
+    lane8 = lax.broadcasted_iota(jnp.int32, (8, NR), 1)
+
+    def column(a, lanes, j):
+        return jnp.broadcast_to(
+            jnp.sum(jnp.where(lanes == j, a, 0.0), axis=1, keepdims=True), a.shape
+        )
+
+    def step(i, carry):
+        k = 4 * i
         a = mat[...]
-        row = mat[pl.ds(k, 1), :]
-        here = lane == k
-        col = jnp.sum(jnp.where(here, a, 0.0), axis=1, keepdims=True)
-        pivot = jnp.sum(jnp.where(lane_row == k, row, 0.0), axis=1, keepdims=True)
-        scaled = jnp.where(lane_row == k, 1.0, row) / pivot
-        new = jnp.where(here, 0.0, a) - col * scaled
-        mat[...] = jnp.where(sub == k, scaled, new)
+        r = [jnp.broadcast_to(mat[pl.ds(k + j, 1), :], (8, NR)) for j in range(4)]
+        c = [column(a, lane, k + j) for j in range(4)]
+        d = [[column(r[m], lane8, k + j) for j in range(4)] for m in range(4)]
+        inside = (lane8 >= k) & (lane8 < k + 4)
+        q = [jnp.where(lane8 == k + j, 1.0, jnp.where(inside, 0.0, r[j])) for j in range(4)]
+        i0 = 1.0 / (d[0][0] * d[1][1] - d[0][1] * d[1][0])
+
+        def lead(x0, x1):
+            return (d[1][1] * x0 - d[0][1] * x1) * i0, (d[0][0] * x1 - d[1][0] * x0) * i0
+
+        e02, e12 = lead(d[0][2], d[1][2])
+        e03, e13 = lead(d[0][3], d[1][3])
+        f0, f1 = lead(q[0], q[1])
+        s22 = d[2][2] - d[2][0] * e02 - d[2][1] * e12
+        s23 = d[2][3] - d[2][0] * e03 - d[2][1] * e13
+        s32 = d[3][2] - d[3][0] * e02 - d[3][1] * e12
+        s33 = d[3][3] - d[3][0] * e03 - d[3][1] * e13
+        g2 = q[2] - d[2][0] * f0 - d[2][1] * f1
+        g3 = q[3] - d[3][0] * f0 - d[3][1] * f1
+        i1 = 1.0 / (s22 * s33 - s23 * s32)
+        w2 = (s33 * g2 - s23 * g3) * i1
+        w3 = (s22 * g3 - s32 * g2) * i1
+        w = [f0 - e02 * w2 - e03 * w3, f1 - e12 * w2 - e13 * w3, w2, w3]
+        w = [x[0:1] for x in w]
+        new = jnp.where((lane >= k) & (lane < k + 4), 0.0, a)
+        new = new - (c[0] * w[0] + c[1] * w[1]) - (c[2] * w[2] + c[3] * w[3])
+        for j in range(4):
+            new = jnp.where(sub == k + j, w[j], new)
+        mat[...] = new
         return carry
 
-    lax.fori_loop(first, last, step, 0)
+    lax.fori_loop(first // 4, last // 4, step, 0)
 
 
 def kernel(
-    schur_h, linv_h, rhs, basis, cmap, cinv, rows, counts,
+    schur_h, linv_h, rhs_h, basis_h, cmap_h, cinv_h, rows_h, counts_h,
     x_out, r_out,
-    schur, linv, perm, weight, mult, sent, got0, got, r0, xw, xz, loc, base,
-    cl_mine, cl_all, map_mine, map_all, e_mine, e_all, coarse, mu, inv,
+    schur, linv, rhs, basis, cmap, cinv, rows, counts, perm, weight, mult, sent, got0, got, r0, xw, xz, loc, base,
+    cl_mine, cl_all, map_mine, map_all, hot, e_mine, e_all, coarse, mu, inv,
     ar_in, ar_r1, ar_p, ar_r2, ar_q, ar_out,
-    load_sem, xs, xr, cs, cr, ms, mr, es, er, as1, ar1, as2, ar2, as3, ar3,
+    load_sem, xs, xr, cs, cr, ms, mr, es, er, as1, ar1, as2, ar2, as3, ar3, as4, ar4,
 ):
     g = lax.axis_index("group")
     s = lax.axis_index("sub")
@@ -94,24 +122,34 @@
         started.append(copy)
         return copy
 
-    load_l = pltpu.make_async_copy(linv_h, linv, load_sem.at[0])
-    load_s = pltpu.make_async_copy(schur_h, schur, load_sem.at[1])
-    load_l.start()
-    load_s.start()
+    pairs = (
+        (cmap_h, cmap), (rhs_h, rhs), (rows_h, rows), (counts_h, counts),
+        (basis_h, basis), (cinv_h, cinv), (linv_h, linv), (schur_h, schur),
+    )
+    loads = [pltpu.make_async_copy(a, b, load_sem.at[i]) for i, (a, b) in enumerate(pairs)]
+    for load in loads:
+        load.start()
+    load_l, load_s = loads[6:]
 
     barrier = pltpu.get_barrier_semaphore()
     mates = [(g, lax.rem(s + k, N_SUB)) for k in range(1, N_SUB)]
     peers = [(lax.rem(g + k, N_GROUP), s) for k in range(1, N_GROUP)]
+    y, z = lax.rem(s, 4), lax.div(s, 4)
+    mates_y = [(g, 4 * z + lax.rem(y + k, 4)) for k in range(1, 4)]
+    mates_z = [(g, 4 * lax.rem(z + k, 4) + y) for k in range(1, 4)]
     for target in mates + peers:
         pl.semaphore_signal(barrier, inc=1, device_id=target, device_id_type=MESH)
 
     map_mine[...] = jnp.zeros((8, NR), jnp.int32)
+    loads[0].wait()
     map_mine[0:1, 0:NC] = cmap[...]
     tile = jnp.broadcast_to(map_mine[0:1, :], (8, NR))
     tile = pltpu.roll(tile, NC * lax.rem(s, 4), 1)
     at_row = lax.broadcasted_iota(jnp.int32, (8, NR), 0) == lax.div(s, 4)
     map_mine[...] = jnp.where(at_row, tile, 0)
 
+    for load in loads[1:6]:
+        load.wait()
     pl.semaphore_wait(barrier, len(mates) + len(peers))
 
     around = [
@@ -136,7 +174,7 @@
     lane = lax.broadcasted_iota(jnp.int32, (1, ZONE), 1)
     at = lax.broadcasted_iota(jnp.int32, (ZONE, ZONE), 0)
     for d in range(4):
-        mine = jnp.where(lane < counts[0, d], rows[0, d : d + 1, :] - ZONE * d, -1)
+        mine = jnp.where(lane < counts[0:1, d : d + 1], rows[0, d : d + 1, :] - ZONE * d, -1)
         theirs = rows[1, d : d + 1, :] - ZONE * (d ^ 1)
         place = jnp.where(at == mine, 1.0, 0.0)
         times = 1.0 + jnp.sum(place, axis=1, keepdims=True)
@@ -145,7 +183,7 @@
         pick = jnp.where(at == theirs, 1.0, 0.0).astype(BF)
         perm[d] = dot(place.astype(BF), pick, ((1,), (1,))).astype(BF)
 
-    for d in range(4):
+    for d in (2, 3, 0, 1):
         copies0[d ^ 1].wait_recv()
         block = rhs[zone(d), :].astype(F32) + dot(perm[d], got0[d])
         r0[zone(d), :] = block
@@ -168,16 +206,15 @@
         for k in range(1, N_SUB):
             total = total + map_all[k]
         at_all = lax.broadcasted_iota(jnp.int32, (NL, NR), 0)
-        at_own = lax.broadcasted_iota(jnp.int32, (OWN_ROWS, NR), 0) + OWN_ROWS * s
-        hot = jnp.concatenate(
-            [jnp.where(at_all == total[i : i + 1, :], 1.0, 0.0).astype(BF) for i in range(4)], axis=1
-        )
-        hot_own = jnp.concatenate(
-            [jnp.where(at_own == total[i : i + 1, :], 1.0, 0.0).astype(BF) for i in range(4)], axis=1
-        )
-        columns = dot(cinv[...], hot).astype(BF)
-        entries = dot(hot_own, columns, ((0,), (0,))).astype(BF)
-        e_mine[...] = entries.reshape(N_SUB, NC, NC_ALL)
+        for i in range(4):
+            hot[:, NR * i : NR * (i + 1)] = jnp.where(
+                at_all == total[i : i + 1, :], 1.0, 0.0
+            ).astype(BF)
+        picks = dot(cinv[...], hot[...]).T
+        picks = jnp.concatenate([picks, picks], axis=1)
+        half = lax.broadcasted_iota(jnp.int32, (NC_ALL, NR), 1) // OWN_ROWS
+        picks = jnp.where(half == lax.rem(s, 2), picks, 0.0).astype(BF)
+        e_mine[...] = picks.reshape(N_SUB, NC, NR)
         copies = [
             remote(
                 e_mine.at[lax.rem(s + k, N_SUB)], e_all.at[s], es.at[k], er.at[k], mates[k - 1]
@@ -186,6 +223,12 @@
         ]
         e_all[s] = e_mine[s]
         return copies
+
+    def coarse_finish(copies):
+        for copy in copies:
+            copy.wait_recv()
+        picks = jnp.concatenate([e_all[2 * i] + e_all[2 * i + 1] for i in range(N_SUB // 2)], axis=1)
+        coarse[...] = dot(picks, hot[...]).astype(BF)
 
     def local_apply(matrix, blocks, d):
         return fold(dot(matrix[zone(d), :], blocks))
@@ -200,12 +243,7 @@
             loc[zone(d), :] = local_apply(linv, blocks, d)
         during()
         if k == 0:
-            for copy in e_copies:
-                copy.wait_recv()
-            total = e_all[0].astype(F32)
-            for i in range(1, N_SUB):
-                total = total + e_all[i].astype(F32)
-            coarse[...] = total.astype(BF)
+            coarse_finish(e_copies)
         for copy in copies:
             copy.wait_recv()
         terms = split(cl_all[k].reshape(NC_ALL, NR))
@@ -230,11 +268,11 @@
         return sent[e - 1, zone(d), :] + fold(dot(perm[d], split(got[e - 1, d])))
 
     def finish_z(k, e, sends):
-        for d in range(4):
+        for d in (2, 3, 0, 1):
             xz[k, zone(d), :] = split(assembled(e, sends, d))
 
     def finish_q(k, e, sends):
-        for d in range(4):
+        for d in (2, 3, 0, 1):
             xw[k + 1, zone(d), :] = split(weight[zone(d), :] * assembled(e, sends, d))
 
     def reduce_start(i):
@@ -248,27 +286,40 @@
         ar_r1[i][g] = ar_in[i][pl.ds(pl.multiple_of(share * g, 8), share), :]
         return copies
 
+    def reduce_spread(i, step, total, targets, send_sem, recv_sem):
+        ar_p[i][step] = total
+        slot = (lax.div(s, 1), lax.rem(s, 4), lax.div(s, 4))[step]
+        copies = [
+            remote(ar_p[i].at[step], ar_r2[i].at[step, slot], send_sem.at[i, k], recv_sem.at[i, k], t)
+            for k, t in enumerate(targets)
+        ]
+        ar_r2[i][step, slot] = total
+        return copies
+
+    def reduce_sum(i, step, waits, count):
+        for copy in waits:
+            copy.wait_recv()
+        total = ar_r2[i][step, 0]
+        for k in range(1, count):
+            total = total + ar_r2[i][step, k]
+        return total
+
     def reduce_middle(i, waits):
         for copy in waits:
             copy.wait_recv()
         total = ar_r1[i][0]
         for k in range(1, N_GROUP):
             total = total + ar_r1[i][k]
-        ar_p[i][...] = total
-        copies = [
-            remote(ar_p[i], ar_r2[i].at[s], as2.at[i, k], ar2.at[i, k], mates[k - 1])
-            for k in range(1, N_SUB)
-        ]
-        ar_r2[i][s] = total
-        return copies
+        if i == 3:
+            return reduce_spread(i, 0, total, mates, as2, ar2)
+        return reduce_spread(i, 1, total, mates_y, as2, ar2)
+
+    def reduce_more(i, waits):
+        return reduce_spread(i, 2, reduce_sum(i, 1, waits, 4), mates_z, as4, ar4)
 
     def reduce_last(i, waits):
         share = AR_ROWS[i] // N_GROUP
-        for copy in waits:
-            copy.wait_recv()
-        total = ar_r2[i][0]
-        for k in range(1, N_SUB):
-            total = total + ar_r2[i][k]
+        total = reduce_sum(i, 0, waits, N_SUB) if i == 3 else reduce_sum(i, 2, waits, 4)
         ar_q[i][...] = total
         mine = pl.ds(pl.multiple_of(share * g, 8), share)
         copies = [
@@ -300,48 +351,49 @@
         state["a"] = reduce_middle(0, state["a"])
 
     sends = precondition(1, 3, during1)
-    state["a"] = reduce_last(0, state["a"])
+    state["a"] = reduce_more(0, state["a"])
     finish_z(1, 3, sends)
     sends = operate(1, 4)
+    state["a"] = reduce_last(0, state["a"])
     ar_in[1][0:NR, :] = gram(xz[1], xw[1])
-    reduce_wait(state["a"])
-    mu[0] = ar_out[0][0:NR, :]
-    inv[0] = sym(ar_out[0][NR:, :])
-    invert_steps(inv.at[0], 0, 32)
     finish_q(1, 4, sends)
     ar_in[1][NR:, :] = gram(xz[1], xw[2])
     state["b"] = reduce_start(1)
 
     def during2():
-        invert_steps(inv.at[0], 32, 64)
+        reduce_wait(state["a"])
+        mu[0] = ar_out[0][0:NR, :]
+        inv[0] = sym(ar_out[0][NR:, :])
+        invert_steps(inv.at[0], 0, 64)
         state["b"] = reduce_middle(1, state["b"])
 
     sends = precondition(2, 5, during2)
-    invert_steps(inv.at[0], 64, 96)
-    state["b"] = reduce_last(1, state["b"])
+    state["b"] = reduce_more(1, state["b"])
+    invert_steps(inv.at[0], 64, 128)
     finish_z(2, 5, sends)
     sends = operate(2, 6)
+    state["b"] = reduce_last(1, state["b"])
     ar_in[2][...] = gram(xz[2], xw[2])
     state["c"] = reduce_start(2)
-    invert_steps(inv.at[0], 96, 128)
     reduce_wait(state["b"])
+    m2 = sym(ar_out[1][0:NR, :])
+    m3 = sym(ar_out[1][NR:, :])
+    inv1 = inv[0]
+    t2 = small(inv1, m2)
+    inv[1] = sym(m3 - small(m2, t2))
     finish_q(2, 6, sends)
     ar_in[3][...] = gram(xz[2], xw[3])
     state["d"] = reduce_start(3)
     state["c"] = reduce_middle(2, state["c"])
     m0 = mu[0]
-    m2 = sym(ar_out[1][0:NR, :])
-    m3 = sym(ar_out[1][NR:, :])
-    inv1 = inv[0]
     t0 = small(inv1, m0)
-    t2 = small(inv1, m2)
     t3 = small(inv1, m3)
-    inv[1] = sym(m3 - small(m2, t2))
     h1 = sym(ar_out[0][NR:, :]) - small(m2, t0)
     state["d"] = reduce_middle(3, state["d"])
-    state["c"] = reduce_last(2, state["c"])
+    state["c"] = reduce_more(2, state["c"])
     invert_steps(inv.at[1], 0, 64)
     state["d"] = reduce_last(3, state["d"])
+    state["c"] = reduce_last(2, state["c"])
     invert_steps(inv.at[1], 64, 128)
     reduce_wait(state["c"])
     m4 = sym(ar_out[2][...])
@@ -387,6 +439,12 @@
     scratch = [
         pltpu.VMEM((NL, NL), BF),
         pltpu.VMEM((NL, NL), BF),
+        pltpu.VMEM((NL, NR), BF),
+        pltpu.VMEM((NC, NL), BF),
+        pltpu.VMEM((1, NC), jnp.int32),
+        pltpu.VMEM((OWN_ROWS, NL), BF),
+        pltpu.VMEM((2, 4, ZONE), jnp.int32),
+        pltpu.VMEM((1, 4), jnp.int32),
         pltpu.VMEM((4, ZONE, ZONE), BF),
         pltpu.VMEM((NL, NR), F32),
         pltpu.VMEM((NL, NR), F32),
@@ -402,18 +460,19 @@
         pltpu.VMEM((3, N_SUB, NC, NR), F32),
         pltpu.VMEM((8, NR), jnp.int32),
         pltpu.VMEM((N_SUB, 8, NR), jnp.int32),
-        pltpu.VMEM((N_SUB, NC, NC_ALL), BF),
-        pltpu.VMEM((N_SUB, NC, NC_ALL), BF),
+        pltpu.VMEM((NL, NC_ALL), BF),
+        pltpu.VMEM((N_SUB, NC, NR), BF),
+        pltpu.VMEM((N_SUB, NC, NR), BF),
         pltpu.VMEM((NC, NC_ALL), BF),
         pltpu.VMEM((1, NR, NR), F32),
         pltpu.VMEM((3, NR, NR), F32),
         [pltpu.VMEM((r, NR), F32) for r in AR_ROWS],
         [pltpu.VMEM((N_GROUP, r, NR), F32) for r in ar_shapes],
-        [pltpu.VMEM((r, NR), F32) for r in ar_shapes],
-        [pltpu.VMEM((N_SUB, r, NR), F32) for r in ar_shapes],
+        [pltpu.VMEM((3, r, NR), F32) for r in ar_shapes],
+        [pltpu.VMEM((3, N_SUB, r, NR), F32) for r in ar_shapes],
         [pltpu.VMEM((r, NR), F32) for r in ar_shapes],
         [pltpu.VMEM((r, NR), F32) for r in AR_ROWS],
-        dma((2,)),
+        dma((8,)),
         dma((7, 4)),
         dma((7, 4)),
         dma((3, N_SUB)),
@@ -428,17 +487,18 @@
         dma((4, N_SUB)),
         dma((4, N_GROUP)),
         dma((4, N_GROUP)),
+        dma((4, 4)),
+        dma((4, 4)),
     ]
     out = jax.ShapeDtypeStruct((NL, NR), F32)
     x, r = pl.pallas_call(
         kernel,
         out_shape=(out, out),
-        in_specs=[anywhere, anywhere, vmem, vmem, vmem, vmem, vmem,
-                  pl.BlockSpec(memory_space=pltpu.SMEM)],
+        in_specs=[anywhere] * 8,
         out_specs=(vmem, vmem),
         scratch_shapes=scratch,
         compiler_params=pltpu.CompilerParams(
-            collective_id=0, has_side_effects=True, vmem_limit_bytes=48 * 1024 * 1024
+            collective_id=0, has_side_effects=True, vmem_limit_bytes=62 * 1024 * 1024
         ),
         name="block_cg",
     )(

time: 129 us -> 108 us (0.84)
  Pallas kernels: 118 us -> 103 us
  local copies, waits for them, and re-layouts: 9.46 us -> 3.74 us
    pallas_call x1, Pallas kernels: 118 us -> 103 us  [shards(): pl.pallas_call(kernel, out_shape=(out, out), in_specs=[anywhere] * 8, out...]
    unnamed x18 -> x2, local copies, waits for them, and re-layouts: 9.46 us -> 3.74 us
where the time goes in v2:
time: 108 us; the launch traced here: 107 us
  Pallas kernels  103 us (95%)
  local copies, waits for them, and re-layouts  3.74 us (3%)
    pallas_call x1, Pallas kernels, shards(): pl.pallas_call(kernel, out_shape=(out, out), in_specs=[anywhere] * 8, out...  103 us
    unnamed x2, local copies, waits for them, and re-layouts  3.74 us

profile of v2, /device:TPU:1, one launch (start us, length us, event | category | flops | bytes accessed | tf_op | source)
XLA Modules:
  0.0 107.4 jit_solution(8802566624752580139)
XLA Ops:
  0.6 103.0 %block_cg.1 = (f32[1024,128]{1,0:T(8,128)}, f32[1024,128]{1,0:T(8,128)}) custom-call(bf16[1024,1024]{1,0:T(8,128)(2,1)} %bitcast.10, bf16[1024,1024]{1,0:T(8,128)(2,1)} %bitcast.11, bf16[1024,128]{1,0:T(8,128)(2,1)} %bitcast.14, bf16[32,1024]{1,0:T(8,128)(2,1)} %bitcast.16, s32[1,32]{1,0:T(1,128)} %bitcast.18, bf16[64,1024]{1,0:T(8,128)(2,1)} %bitcast.15, ...), custom_call_target="tpu_custom_call" | custom-call | tf_op jit(solution)/shard_map/block_cg/pallas_call | solution.py:494
  103.7 1.9 %copy.12 = f32[1,1,1024,128]{3,2,1,0:T(8,128)} copy(f32[1,1,1024,128]{3,2,1,0:T(8,128)} %bitcast.13) | data formatting | bytes 1048576
  105.5 1.9 %copy.13 = f32[1,1,1024,128]{3,2,1,0:T(8,128)} copy(f32[1,1,1024,128]{3,2,1,0:T(8,128)} %bitcast.12) | data formatting | bytes 1048576

commit v3 on v2

--- a/solution.py
+++ b/solution.py
@@ -18,6 +18,7 @@
 NC = 32
 NC_ALL = NC * N_SUB
 OWN_ROWS = 64
+HALF = NR // 2
 AR_ROWS = (256, 256, 128, 128)
 
 
@@ -55,8 +56,8 @@
 
 
 def invert_steps(mat, first, last):
-    lane = lax.broadcasted_iota(jnp.int32, (NR, NR), 1)
-    sub = lax.broadcasted_iota(jnp.int32, (NR, NR), 0)
+    lane = lax.broadcasted_iota(jnp.int32, (HALF, NR), 1)
+    sub = lax.broadcasted_iota(jnp.int32, (HALF, NR), 0)
     lane8 = lax.broadcasted_iota(jnp.int32, (8, NR), 1)
 
     def column(a, lanes, j):
@@ -101,13 +102,40 @@
     lax.fori_loop(first // 4, last // 4, step, 0)
 
 
+def small_t(a, b):
+    return lax.dot_general(
+        a, b, (((0,), (0,)), ((), ())), precision=lax.Precision.HIGHEST, preferred_element_type=F32
+    )
+
+
+def invert_lead(top, mat):
+    top[...] = mat[0:HALF, :]
+
+
+def invert_next(top, bottom, mat):
+    rest = mat[HALF:, HALF:] - small_t(mat[0:HALF, HALF:], top[:, HALF:])
+    bottom[...] = jnp.concatenate([rest, jnp.zeros((HALF, HALF), F32)], axis=1)
+
+
+def invert_end(top, bottom):
+    x = top[:, HALF:]
+    low = bottom[:, :HALF]
+    xl = small(x, low)
+    corner = top[:, :HALF] + lax.dot_general(
+        xl, x, (((1,), (1,)), ((), ())), precision=lax.Precision.HIGHEST, preferred_element_type=F32
+    )
+    upper = jnp.concatenate([corner, -xl], axis=1)
+    lower = jnp.concatenate([-xl.T, low], axis=1)
+    return jnp.concatenate([upper, lower], axis=0)
+
+
 def kernel(
     schur_h, linv_h, rhs_h, basis_h, cmap_h, cinv_h, rows_h, counts_h,
     x_out, r_out,
     schur, linv, rhs, basis, cmap, cinv, rows, counts, perm, weight, mult, sent, got0, got, r0, xw, xz, loc, base,
-    cl_mine, cl_all, map_mine, map_all, hot, e_mine, e_all, coarse, mu, inv,
+    cl_mine, cl_all, map_mine, map_all, hot, e_mine, e_all, coarse, mat, top, bottom, g_mine, g_all, ct_mine, ct_all, pk_mine, pk_all,
     ar_in, ar_r1, ar_p, ar_r2, ar_q, ar_out,
-    load_sem, xs, xr, cs, cr, ms, mr, es, er, as1, ar1, as2, ar2, as3, ar3, as4, ar4,
+    load_sem, xs, xr, cs, cr, ms, mr, es, er, as1, ar1, as2, ar2, as3, ar3, as4, ar4, gs, gr, ts, tr, ps, pr,
 ):
     g = lax.axis_index("group")
     s = lax.axis_index("sub")
@@ -119,8 +147,15 @@
             device_id=target, device_id_type=MESH,
         )
         copy.start()
-        started.append(copy)
-        return copy
+
+    def arrived(span, sem):
+        pltpu.make_async_copy(span, span, sem).wait()
+
+    def transfer(copies, span, send_sem, recv_sem):
+        for src, dst, target in copies:
+            remote(src, dst, send_sem, recv_sem, target)
+        started.append((span, send_sem))
+        return span, recv_sem
 
     pairs = (
         (cmap_h, cmap), (rhs_h, rhs), (rows_h, rows), (counts_h, counts),
@@ -160,16 +195,23 @@
     ]
 
     def send_zone(e, d, src, dst):
-        return remote(src, dst.at[d ^ 1], xs.at[e, d], xr.at[e, d ^ 1], around[d])
+        remote(src, dst.at[d ^ 1], xs.at[e], xr.at[e, d ^ 1], around[d])
+        if d == 3:
+            started.append((dst, xs.at[e]))
+
+    def zone_arrived(e, d):
+        zones = got0 if e == 0 else got.at[e - 1]
+        arrived(zones.at[d], xr.at[e, d])
 
     def zone(d):
         return pl.ds(ZONE * d, ZONE)
 
-    copies0 = [send_zone(0, d, rhs.at[zone(d)], got0) for d in range(4)]
-    map_copies = [
-        remote(map_mine, map_all.at[k], ms.at[k], mr.at[k], mates[k - 1])
-        for k in range(1, N_SUB)
-    ]
+    for d in range(4):
+        send_zone(0, d, rhs.at[zone(d)], got0)
+    map_sent = transfer(
+        [(map_mine, map_all.at[k], mates[k - 1]) for k in range(1, N_SUB)],
+        map_all.at[pl.ds(0, N_SUB - 1)], ms.at[0], mr.at[0],
+    )
 
     lane = lax.broadcasted_iota(jnp.int32, (1, ZONE), 1)
     at = lax.broadcasted_iota(jnp.int32, (ZONE, ZONE), 0)
@@ -181,27 +223,30 @@
         mult[zone(d), :] = jnp.broadcast_to(times, (ZONE, NR))
         weight[zone(d), :] = jnp.broadcast_to(1.0 / times, (ZONE, NR))
         pick = jnp.where(at == theirs, 1.0, 0.0).astype(BF)
-        perm[d] = dot(place.astype(BF), pick, ((1,), (1,))).astype(BF)
+        pairs_d = dot(place.astype(BF), pick, ((1,), (1,)))
+        perm[d] = pairs_d.astype(BF)
+        shared = (pairs_d * (1.0 / times)).astype(BF)
+        g_mine[d] = dot(basis[:, zone(d)], shared).astype(BF)
+    g_sent = transfer(
+        [(g_mine.at[d], g_all.at[d ^ 1], around[d]) for d in range(4)], g_all, gs.at[0], gr.at[0]
+    )
 
     for d in (2, 3, 0, 1):
-        copies0[d ^ 1].wait_recv()
+        zone_arrived(0, d)
         block = rhs[zone(d), :].astype(F32) + dot(perm[d], got0[d])
         r0[zone(d), :] = block
         xw[0, zone(d), :] = split(weight[zone(d), :] * block)
 
-    def coarse_send(k):
-        local = fold(dot(basis[...], xw[k]))
+    def coarse_send(k, local):
         cl_mine[k] = local
-        copies = [
-            remote(cl_mine.at[k], cl_all.at[k, s], cs.at[k, i + 1], cr.at[k, i + 1], mates[i])
-            for i in range(N_SUB - 1)
-        ]
         cl_all[k, s] = local
-        return copies
+        return transfer(
+            [(cl_mine.at[k], cl_all.at[k, s], t) for t in mates],
+            cl_all.at[k, pl.ds(0, N_SUB - 1)], cs.at[k], cr.at[k],
+        )
 
     def coarse_setup():
-        for copy in map_copies:
-            copy.wait_recv()
+        arrived(*map_sent)
         total = map_mine[...]
         for k in range(1, N_SUB):
             total = total + map_all[k]
@@ -215,98 +260,107 @@
         half = lax.broadcasted_iota(jnp.int32, (NC_ALL, NR), 1) // OWN_ROWS
         picks = jnp.where(half == lax.rem(s, 2), picks, 0.0).astype(BF)
         e_mine[...] = picks.reshape(N_SUB, NC, NR)
-        copies = [
-            remote(
-                e_mine.at[lax.rem(s + k, N_SUB)], e_all.at[s], es.at[k], er.at[k], mates[k - 1]
-            )
-            for k in range(1, N_SUB)
-        ]
         e_all[s] = e_mine[s]
-        return copies
-
-    def coarse_finish(copies):
-        for copy in copies:
-            copy.wait_recv()
+        return transfer(
+            [
+                (e_mine.at[lax.rem(s + k, N_SUB)], e_all.at[s], mates[k - 1])
+                for k in range(1, N_SUB)
+            ],
+            e_all.at[pl.ds(0, N_SUB - 1)], es.at[0], er.at[0],
+        )
+
+    def coarse_finish(e_sent):
+        arrived(*e_sent)
         picks = jnp.concatenate([e_all[2 * i] + e_all[2 * i + 1] for i in range(N_SUB // 2)], axis=1)
         coarse[...] = dot(picks, hot[...]).astype(BF)
 
     def local_apply(matrix, blocks, d):
         return fold(dot(matrix[zone(d), :], blocks))
 
-    def precondition(k, e, during):
-        copies = coarse_send(k)
-        if k == 0:
-            e_copies = coarse_setup()
-            load_l.wait()
+    def local_part(k, e):
         blocks = xw[k]
         for d in range(4):
-            loc[zone(d), :] = local_apply(linv, blocks, d)
-        during()
-        if k == 0:
-            coarse_finish(e_copies)
-        for copy in copies:
-            copy.wait_recv()
+            sent[e - 1, zone(d), :] = weight[zone(d), :] * local_apply(linv, blocks, d)
+            send_zone(e, d, sent.at[e - 1, zone(d)], got.at[e - 1])
+
+    def coarse_part(k, e, gathered):
+        arrived(*gathered)
         terms = split(cl_all[k].reshape(NC_ALL, NR))
-        picked = split(fold(dot(coarse[...], terms)))
-        sends = []
+        values = fold(dot(coarse[...], terms))
+        pk_mine[k] = values
+        values_sent = transfer(
+            [(pk_mine.at[k], pk_all.at[k, d ^ 1], around[d]) for d in range(4)],
+            pk_all.at[k], ps.at[k], pr.at[k],
+        )
+        picked = split(values)
         for d in range(4):
             part = fold(dot(basis[:, zone(d)], picked, ((0,), (0,))))
-            sent[e - 1, zone(d), :] = weight[zone(d), :] * (loc[zone(d), :] + part)
-            sends.append(send_zone(e, d, sent.at[e - 1, zone(d)], got.at[e - 1]))
-        return sends
-
-    def operate(k, e):
-        sends = []
+            loc[zone(d), :] = sent[e - 1, zone(d), :] + weight[zone(d), :] * part
+        return values_sent
+
+    def finish_z(k, e, values_sent):
+        arrived(*values_sent)
+        for d in (2, 3, 0, 1):
+            theirs = fold(dot(g_all[d], split(pk_all[k, d]), ((0,), (0,))))
+            mine = loc[zone(d), :] + theirs
+            zone_arrived(e, d)
+            xz[k, zone(d), :] = split(mine + fold(dot(perm[d], split(got[e - 1, d]))))
+
+    def operate(k, e, coarse_too):
         blocks = xz[k]
         for d in range(4):
-            sent[e - 1, zone(d), :] = local_apply(schur, blocks, d)
-            sends.append(send_zone(e, d, sent.at[e - 1, zone(d)], got.at[e - 1]))
-        return sends
-
-    def assembled(e, sends, d):
-        sends[d ^ 1].wait_recv()
-        return sent[e - 1, zone(d), :] + fold(dot(perm[d], split(got[e - 1, d])))
-
-    def finish_z(k, e, sends):
+            image = local_apply(schur, blocks, d)
+            sent[e - 1, zone(d), :] = image
+            if coarse_too:
+                ct_mine[k, d] = fold(dot(g_all[d], split(image)))
+                remote(ct_mine.at[k, d], ct_all.at[k, d ^ 1], ts.at[k], tr.at[k], around[d])
+            send_zone(e, d, sent.at[e - 1, zone(d)], got.at[e - 1])
+        if coarse_too:
+            started.append((ct_all.at[k], ts.at[k]))
+
+    def coarse_shares(k, e):
+        total = fold(dot(basis[...], split(weight[...] * sent[e - 1])))
+        arrived(ct_all.at[k], tr.at[k])
+        for d in range(4):
+            total = total + ct_all[k, d]
+        return coarse_send(k + 1, total)
+
+    def finish_q(k, e):
         for d in (2, 3, 0, 1):
-            xz[k, zone(d), :] = split(assembled(e, sends, d))
-
-    def finish_q(k, e, sends):
-        for d in (2, 3, 0, 1):
-            xw[k + 1, zone(d), :] = split(weight[zone(d), :] * assembled(e, sends, d))
+            zone_arrived(e, d)
+            whole = sent[e - 1, zone(d), :] + fold(dot(perm[d], split(got[e - 1, d])))
+            xw[k + 1, zone(d), :] = split(weight[zone(d), :] * whole)
 
     def reduce_start(i):
         share = AR_ROWS[i] // N_GROUP
-        copies = []
-        for k in range(1, N_GROUP):
-            src = ar_in[i].at[pl.ds(pl.multiple_of(share * peers[k - 1][0], 8), share)]
-            copies.append(
-                remote(src, ar_r1[i].at[g], as1.at[i, k], ar1.at[i, k], peers[k - 1])
-            )
-        ar_r1[i][g] = ar_in[i][pl.ds(pl.multiple_of(share * g, 8), share), :]
-        return copies
+
+        def part(t):
+            return pl.ds(pl.multiple_of(share * t, 8), share)
+
+        ar_r1[i][g] = ar_in[i][part(g), :]
+        return transfer(
+            [(ar_in[i].at[part(t[0])], ar_r1[i].at[g], t) for t in peers],
+            ar_r1[i].at[pl.ds(0, N_GROUP - 1)], as1.at[i], ar1.at[i],
+        )
 
     def reduce_spread(i, step, total, targets, send_sem, recv_sem):
         ar_p[i][step] = total
-        slot = (lax.div(s, 1), lax.rem(s, 4), lax.div(s, 4))[step]
-        copies = [
-            remote(ar_p[i].at[step], ar_r2[i].at[step, slot], send_sem.at[i, k], recv_sem.at[i, k], t)
-            for k, t in enumerate(targets)
-        ]
+        slot = (s, lax.rem(s, 4), lax.div(s, 4))[step]
         ar_r2[i][step, slot] = total
-        return copies
+        return transfer(
+            [(ar_p[i].at[step], ar_r2[i].at[step, slot], t) for t in targets],
+            ar_r2[i].at[step, pl.ds(0, len(targets))], send_sem.at[i], recv_sem.at[i],
+        )
 
     def reduce_sum(i, step, waits, count):
-        for copy in waits:
-            copy.wait_recv()
+        arrived(*waits)
         total = ar_r2[i][step, 0]
         for k in range(1, count):
             total = total + ar_r2[i][step, k]
         return total
 
     def reduce_middle(i, waits):
-        for copy in waits:
-            copy.wait_recv()
+        arrived(*waits)
         total = ar_r1[i][0]
         for k in range(1, N_GROUP):
             total = total + ar_r1[i][k]
@@ -322,91 +376,92 @@
         total = reduce_sum(i, 0, waits, N_SUB) if i == 3 else reduce_sum(i, 2, waits, 4)
         ar_q[i][...] = total
         mine = pl.ds(pl.multiple_of(share * g, 8), share)
-        copies = [
-            remote(ar_q[i], ar_out[i].at[mine], as3.at[i, k], ar3.at[i, k], peers[k - 1])
-            for k in range(1, N_GROUP)
-        ]
         ar_out[i][mine, :] = total
-        return copies
+        return transfer(
+            [(ar_q[i], ar_out[i].at[mine], t) for t in peers],
+            ar_out[i].at[pl.ds(0, share * (N_GROUP - 1))], as3.at[i], ar3.at[i],
+        )
 
     def reduce_wait(waits):
-        for copy in waits:
-            copy.wait_recv()
-
-    def nothing():
-        pass
-
-    state = {}
-
-    sends = precondition(0, 1, nothing)
-    finish_z(0, 1, sends)
+        arrived(*waits)
+
+    gathered = coarse_send(0, fold(dot(basis[...], xw[0])))
+    e_sent = coarse_setup()
+    load_l.wait()
+    local_part(0, 1)
+    arrived(*g_sent)
+    coarse_finish(e_sent)
+    values_sent = coarse_part(0, 1, gathered)
     load_s.wait()
-    sends = operate(0, 2)
+    finish_z(0, 1, values_sent)
+
+    operate(0, 2, True)
+    gathered = coarse_shares(0, 2)
     ar_in[0][0:NR, :] = gram(xz[0], xw[0])
-    finish_q(0, 2, sends)
+    finish_q(0, 2)
+    local_part(1, 3)
     ar_in[0][NR:, :] = gram(xz[0], xw[1])
-    state["a"] = reduce_start(0)
-
-    def during1():
-        state["a"] = reduce_middle(0, state["a"])
-
-    sends = precondition(1, 3, during1)
-    state["a"] = reduce_more(0, state["a"])
-    finish_z(1, 3, sends)
-    sends = operate(1, 4)
-    state["a"] = reduce_last(0, state["a"])
+    ar_a = reduce_start(0)
+    values_sent = coarse_part(1, 3, gathered)
+    ar_a = reduce_middle(0, ar_a)
+    finish_z(1, 3, values_sent)
+
+    operate(1, 4, True)
+    ar_a = reduce_more(0, ar_a)
+    gathered = coarse_shares(1, 4)
     ar_in[1][0:NR, :] = gram(xz[1], xw[1])
-    finish_q(1, 4, sends)
+    ar_a = reduce_last(0, ar_a)
+    finish_q(1, 4)
+    local_part(2, 5)
     ar_in[1][NR:, :] = gram(xz[1], xw[2])
-    state["b"] = reduce_start(1)
-
-    def during2():
-        reduce_wait(state["a"])
-        mu[0] = ar_out[0][0:NR, :]
-        inv[0] = sym(ar_out[0][NR:, :])
-        invert_steps(inv.at[0], 0, 64)
-        state["b"] = reduce_middle(1, state["b"])
-
-    sends = precondition(2, 5, during2)
-    state["b"] = reduce_more(1, state["b"])
-    invert_steps(inv.at[0], 64, 128)
-    finish_z(2, 5, sends)
-    sends = operate(2, 6)
-    state["b"] = reduce_last(1, state["b"])
+    ar_b = reduce_start(1)
+    reduce_wait(ar_a)
+    mat[0] = sym(ar_out[0][NR:, :])
+    invert_lead(top.at[0], mat.at[0])
+    invert_steps(top.at[0], 0, 32)
+    values_sent = coarse_part(2, 5, gathered)
+    ar_b = reduce_middle(1, ar_b)
+    invert_steps(top.at[0], 32, 64)
+    invert_next(top.at[0], bottom.at[0], mat.at[0])
+    finish_z(2, 5, values_sent)
+
+    operate(2, 6, False)
     ar_in[2][...] = gram(xz[2], xw[2])
-    state["c"] = reduce_start(2)
-    reduce_wait(state["b"])
+    ar_c = reduce_start(2)
+    ar_b = reduce_more(1, ar_b)
+    invert_steps(bottom.at[0], 0, 64)
+    inv1 = invert_end(top.at[0], bottom.at[0])
+    m0 = ar_out[0][0:NR, :]
+    ar_b = reduce_last(1, ar_b)
+    t0 = small(inv1, m0)
+    finish_q(2, 6)
+    ar_in[3][...] = gram(xz[2], xw[3])
+    ar_d = reduce_start(3)
+    ar_c = reduce_middle(2, ar_c)
+    reduce_wait(ar_b)
     m2 = sym(ar_out[1][0:NR, :])
     m3 = sym(ar_out[1][NR:, :])
-    inv1 = inv[0]
     t2 = small(inv1, m2)
-    inv[1] = sym(m3 - small(m2, t2))
-    finish_q(2, 6, sends)
-    ar_in[3][...] = gram(xz[2], xw[3])
-    state["d"] = reduce_start(3)
-    state["c"] = reduce_middle(2, state["c"])
-    m0 = mu[0]
-    t0 = small(inv1, m0)
+    mat[1] = sym(m3 - small(m2, t2))
+    invert_lead(top.at[1], mat.at[1])
+    ar_d = reduce_middle(3, ar_d)
+    ar_c = reduce_more(2, ar_c)
+    invert_steps(top.at[1], 0, 64)
+    invert_next(top.at[1], bottom.at[1], mat.at[1])
+    ar_c = reduce_last(2, ar_c)
+    invert_steps(bottom.at[1], 0, 32)
+    ar_d = reduce_last(3, ar_d)
+    invert_steps(bottom.at[1], 32, 64)
+    inv2 = invert_end(top.at[1], bottom.at[1])
     t3 = small(inv1, m3)
-    h1 = sym(ar_out[0][NR:, :]) - small(m2, t0)
-    state["d"] = reduce_middle(3, state["d"])
-    state["c"] = reduce_more(2, state["c"])
-    invert_steps(inv.at[1], 0, 64)
-    state["d"] = reduce_last(3, state["d"])
-    state["c"] = reduce_last(2, state["c"])
-    invert_steps(inv.at[1], 64, 128)
-    reduce_wait(state["c"])
+    h1 = mat[0] - small(m2, t0)
+    reduce_wait(ar_c)
     m4 = sym(ar_out[2][...])
-    inv2 = inv[1]
     s23 = m4 - small(m2, t3)
     y = small(inv2, s23)
     u1 = small(inv2, h1)
-    h2 = m2 - small(m3, t0) - lax.dot_general(
-        s23, u1, (((0,), (0,)), ((), ())), precision=lax.Precision.HIGHEST, preferred_element_type=F32
-    )
-    part = small(m3, t3) + lax.dot_general(
-        s23, y, (((0,), (0,)), ((), ())), precision=lax.Precision.HIGHEST, preferred_element_type=F32
-    )
+    h2 = m2 - small(m3, t0) - small_t(s23, u1)
+    part = small(m3, t3) + small_t(s23, y)
     a0 = t0 - small(t2, u1)
     d0 = small(t2, y) - t3
     x_out[...] = combine(xz[0], a0) + combine(xz[1], u1)
@@ -419,21 +474,28 @@
     base[1] = split(
         qd[:, :NR].astype(F32) + qd[:, NR:].astype(F32) - combine(xw[2], y) + combine(xw[1], d0)
     )
-    reduce_wait(state["d"])
-    inv[2] = sym(ar_out[3][...] - part)
-    invert_steps(inv.at[2], 0, 128)
-    c2 = small(inv[2], h2)
+    reduce_wait(ar_d)
+    mat[2] = sym(ar_out[3][...] - part)
+    invert_lead(top.at[2], mat.at[2])
+    invert_steps(top.at[2], 0, 64)
+    invert_next(top.at[2], bottom.at[2], mat.at[2])
+    cross = top[2, :, HALF:]
+    above = small(top[2, :, :HALF], h2[:HALF])
+    below = h2[HALF:] - small_t(cross, h2[:HALF])
+    invert_steps(bottom.at[2], 0, 64)
+    below = small(bottom[2, :, :HALF], below)
+    c2 = jnp.concatenate([above - small(cross, below), below], axis=0)
     x_out[...] = x_out[...] + combine(base[0], c2)
     r_out[...] = r_out[...] - mult[...] * combine(base[1], c2)
-    for copy in started:
-        copy.wait_send()
+    for span, sem in started:
+        arrived(span, sem)
 
 
 def shards(
     schur, local_inverse, rhs_parts, basis, coarse_map, coarse_inverse, shared_rows, shared_counts
 ):
     vmem = pl.BlockSpec(memory_space=pltpu.VMEM)
-    anywhere = pl.BlockSpec(memory_space=pl.ANY)
+    in_hbm = pl.BlockSpec(memory_space=pl.ANY)
     dma = pltpu.SemaphoreType.DMA
     ar_shapes = [r // N_GROUP for r in AR_ROWS]
     scratch = [
@@ -464,8 +526,15 @@
         pltpu.VMEM((N_SUB, NC, NR), BF),
         pltpu.VMEM((N_SUB, NC, NR), BF),
         pltpu.VMEM((NC, NC_ALL), BF),
-        pltpu.VMEM((1, NR, NR), F32),
         pltpu.VMEM((3, NR, NR), F32),
+        pltpu.VMEM((3, HALF, NR), F32),
+        pltpu.VMEM((3, HALF, NR), F32),
+        pltpu.VMEM((4, NC, ZONE), BF),
+        pltpu.VMEM((4, NC, ZONE), BF),
+        pltpu.VMEM((2, 4, NC, NR), F32),
+        pltpu.VMEM((2, 4, NC, NR), F32),
+        pltpu.VMEM((3, NC, NR), F32),
+        pltpu.VMEM((3, 4, NC, NR), F32),
         [pltpu.VMEM((r, NR), F32) for r in AR_ROWS],
         [pltpu.VMEM((N_GROUP, r, NR), F32) for r in ar_shapes],
         [pltpu.VMEM((3, r, NR), F32) for r in ar_shapes],
@@ -473,28 +542,34 @@
         [pltpu.VMEM((r, NR), F32) for r in ar_shapes],
         [pltpu.VMEM((r, NR), F32) for r in AR_ROWS],
         dma((8,)),
+        dma((7,)),
         dma((7, 4)),
-        dma((7, 4)),
-        dma((3, N_SUB)),
-        dma((3, N_SUB)),
-        dma((N_SUB,)),
-        dma((N_SUB,)),
-        dma((N_SUB,)),
-        dma((N_SUB,)),
-        dma((4, N_GROUP)),
-        dma((4, N_GROUP)),
-        dma((4, N_SUB)),
-        dma((4, N_SUB)),
-        dma((4, N_GROUP)),
-        dma((4, N_GROUP)),
-        dma((4, 4)),
-        dma((4, 4)),
+        dma((3,)),
+        dma((3,)),
+        dma((1,)),
+        dma((1,)),
+        dma((1,)),
+        dma((1,)),
+        dma((4,)),
+        dma((4,)),
+        dma((4,)),
+        dma((4,)),
+        dma((4,)),
+        dma((4,)),
+        dma((4,)),
+        dma((4,)),
+        dma((1,)),
+        dma((1,)),
+        dma((2,)),
+        dma((2,)),
+        dma((3,)),
+        dma((3,)),
     ]
     out = jax.ShapeDtypeStruct((NL, NR), F32)
     x, r = pl.pallas_call(
         kernel,
         out_shape=(out, out),
-        in_specs=[anywhere] * 8,
+        in_specs=[in_hbm] * 8,
         out_specs=(vmem, vmem),
         scratch_shapes=scratch,
         compiler_params=pltpu.CompilerParams(

time: 108 us -> 97.4 us (0.902)
  Pallas kernels: 103 us -> 92.8 us
    pallas_call x1, Pallas kernels: 103 us -> 92.8 us  [shards(): pl.pallas_call(kernel, out_shape=(out, out), in_specs=[in_hbm] * 8, out_s...]
where the time goes in v3:
time: 97.4 us; the launch traced here: 97.2 us
  Pallas kernels  92.8 us (95%)
  local copies, waits for them, and re-layouts  3.74 us (4%)
    pallas_call x1, Pallas kernels, shards(): pl.pallas_call(kernel, out_shape=(out, out), in_specs=[in_hbm] * 8, out_s...  92.8 us
    unnamed x2, local copies, waits for them, and re-layouts  3.74 us

profile of v3, /device:TPU:1, one launch (start us, length us, event | category | flops | bytes accessed | tf_op | source)
XLA Modules:
  0.0 97.2 jit_solution(9319315309854341500)
XLA Ops:
  0.6 92.8 %block_cg.1 = (f32[1024,128]{1,0:T(8,128)}, f32[1024,128]{1,0:T(8,128)}) custom-call(bf16[1024,1024]{1,0:T(8,128)(2,1)} %bitcast.10, bf16[1024,1024]{1,0:T(8,128)(2,1)} %bitcast.11, bf16[1024,128]{1,0:T(8,128)(2,1)} %bitcast.14, bf16[32,1024]{1,0:T(8,128)(2,1)} %bitcast.16, s32[1,32]{1,0:T(1,128)} %bitcast.18, bf16[64,1024]{1,0:T(8,128)(2,1)} %bitcast.15, ...), custom_call_target="tpu_custom_call" | custom-call | tf_op jit(solution)/shard_map/block_cg/pallas_call | solution.py:569
  93.5 1.9 %copy.12 = f32[1,1,1024,128]{3,2,1,0:T(8,128)} copy(f32[1,1,1024,128]{3,2,1,0:T(8,128)} %bitcast.13) | data formatting | bytes 1048576
  95.4 1.9 %copy.13 = f32[1,1,1024,128]{3,2,1,0:T(8,128)} copy(f32[1,1,1024,128]{3,2,1,0:T(8,128)} %bitcast.12) | data formatting | bytes 1048576

commit v4 on v3

--- a/solution.py
+++ b/solution.py
@@ -132,10 +132,10 @@
 def kernel(
     schur_h, linv_h, rhs_h, basis_h, cmap_h, cinv_h, rows_h, counts_h,
     x_out, r_out,
-    schur, linv, rhs, basis, cmap, cinv, rows, counts, perm, weight, mult, sent, got0, got, r0, xw, xz, loc, base,
-    cl_mine, cl_all, map_mine, map_all, hot, e_mine, e_all, coarse, mat, top, bottom, g_mine, g_all, ct_mine, ct_all, pk_mine, pk_all,
+    schur, linv, rhs, basis, cmap, cinv, rows, counts, perm, weight, mult, sent, coded, step_mine, step_all, got0, got, r0, xw, xz, loc, base,
+    cl_mine, cl_all, map_mine, map_all, hot, e_mine, e_all, coarse, mat, top, bottom, g_mine, g_all, ct_mine, ct_all, gs_rows, own_share, pk_mine, pk_all,
     ar_in, ar_r1, ar_p, ar_r2, ar_q, ar_out,
-    load_sem, xs, xr, cs, cr, ms, mr, es, er, as1, ar1, as2, ar2, as3, ar3, as4, ar4, gs, gr, ts, tr, ps, pr,
+    load_sem, xs, xr, cs, cr, ms, mr, es, er, as1, ar1, as2, ar2, as3, ar3, as4, ar4, gs, gr, ts, tr, ps, pr, qs, qr,
 ):
     g = lax.axis_index("group")
     s = lax.axis_index("sub")
@@ -198,6 +198,27 @@
         remote(src, dst.at[d ^ 1], xs.at[e], xr.at[e, d ^ 1], around[d])
         if d == 3:
             started.append((dst, xs.at[e]))
+
+    def ship(e, d, value):
+        sent[e - 1, zone(d), :] = value
+        top_value = jnp.maximum(jnp.max(jnp.abs(value), axis=0, keepdims=True), 2e-34)
+        step_mine[e - 1, d] = jnp.broadcast_to(top_value * (1.0 / 32767.0), (8, NR))
+        remote(
+            step_mine.at[e - 1, d], step_all.at[e - 1, d ^ 1], qs.at[e - 1], qr.at[e - 1], around[d]
+        )
+        if d == 3:
+            started.append((step_all.at[e - 1], qs.at[e - 1]))
+        steps = jnp.round(value * (32767.0 / top_value))
+        coded[e - 1, zone(d), :] = steps.astype(jnp.int32).astype(jnp.int16)
+        send_zone(e, d, coded.at[e - 1, zone(d)], got.at[e - 1])
+
+    def steps_arrived(e):
+        arrived(step_all.at[e - 1], qr.at[e - 1])
+
+    def shipped(e, d):
+        zone_arrived(e, d)
+        steps = got[e - 1, d].astype(jnp.int32).astype(F32)
+        return fold(dot(perm[d], split(steps))) * step_all[e - 1, d, 0:1, :]
 
     def zone_arrived(e, d):
         zones = got0 if e == 0 else got.at[e - 1]
@@ -280,8 +301,7 @@
     def local_part(k, e):
         blocks = xw[k]
         for d in range(4):
-            sent[e - 1, zone(d), :] = weight[zone(d), :] * local_apply(linv, blocks, d)
-            send_zone(e, d, sent.at[e - 1, zone(d)], got.at[e - 1])
+            ship(e, d, weight[zone(d), :] * local_apply(linv, blocks, d))
 
     def coarse_part(k, e, gathered):
         arrived(*gathered)
@@ -300,35 +320,55 @@
 
     def finish_z(k, e, values_sent):
         arrived(*values_sent)
+        steps_arrived(e)
         for d in (2, 3, 0, 1):
             theirs = fold(dot(g_all[d], split(pk_all[k, d]), ((0,), (0,))))
             mine = loc[zone(d), :] + theirs
-            zone_arrived(e, d)
-            xz[k, zone(d), :] = split(mine + fold(dot(perm[d], split(got[e - 1, d]))))
+            xz[k, zone(d), :] = split(mine + shipped(e, d))
+
+    def shares_setup():
+        row = lax.broadcasted_iota(jnp.int32, (ZONE, ZONE), 0)
+        column = lax.broadcasted_iota(jnp.int32, (ZONE, ZONE), 1)
+        own = jnp.zeros((NC, NL), F32)
+        for d in range(4):
+            both = jnp.concatenate([weight[zone(d), :], weight[zone(d), :]], axis=1)
+            scaled = dot(basis[:, zone(d)], jnp.where(row == column, both, 0.0).astype(BF)).astype(BF)
+            own = own + dot(scaled, schur[zone(d), :])
+            put_rows(d, dot(g_all[d], schur[zone(d), :]))
+        put_rows(4, own)
+
+    def put_rows(i, rows_f):
+        hi = rows_f.astype(BF)
+        gs_rows[pl.ds(2 * NC * i, NC), :] = hi
+        gs_rows[pl.ds(2 * NC * i + NC, NC), :] = (rows_f - hi.astype(F32)).astype(BF)
 
     def operate(k, e, coarse_too):
         blocks = xz[k]
+        if coarse_too:
+            terms = fold(dot(gs_rows[...], blocks))
+            terms = [
+                terms[2 * NC * i : 2 * NC * i + NC] + terms[2 * NC * i + NC : 2 * NC * (i + 1)]
+                for i in range(5)
+            ]
+            for d in range(4):
+                ct_mine[k, d] = terms[d]
+                remote(ct_mine.at[k, d], ct_all.at[k, d ^ 1], ts.at[k], tr.at[k], around[d])
+            started.append((ct_all.at[k], ts.at[k]))
+            own_share[...] = terms[4]
         for d in range(4):
-            image = local_apply(schur, blocks, d)
-            sent[e - 1, zone(d), :] = image
-            if coarse_too:
-                ct_mine[k, d] = fold(dot(g_all[d], split(image)))
-                remote(ct_mine.at[k, d], ct_all.at[k, d ^ 1], ts.at[k], tr.at[k], around[d])
-            send_zone(e, d, sent.at[e - 1, zone(d)], got.at[e - 1])
-        if coarse_too:
-            started.append((ct_all.at[k], ts.at[k]))
+            ship(e, d, local_apply(schur, blocks, d))
 
     def coarse_shares(k, e):
-        total = fold(dot(basis[...], split(weight[...] * sent[e - 1])))
+        total = own_share[...]
         arrived(ct_all.at[k], tr.at[k])
         for d in range(4):
             total = total + ct_all[k, d]
         return coarse_send(k + 1, total)
 
     def finish_q(k, e):
+        steps_arrived(e)
         for d in (2, 3, 0, 1):
-            zone_arrived(e, d)
-            whole = sent[e - 1, zone(d), :] + fold(dot(perm[d], split(got[e - 1, d])))
+            whole = sent[e - 1, zone(d), :] + shipped(e, d)
             xw[k + 1, zone(d), :] = split(weight[zone(d), :] * whole)
 
     def reduce_start(i):
@@ -390,9 +430,10 @@
     load_l.wait()
     local_part(0, 1)
     arrived(*g_sent)
+    load_s.wait()
+    shares_setup()
     coarse_finish(e_sent)
     values_sent = coarse_part(0, 1, gathered)
-    load_s.wait()
     finish_z(0, 1, values_sent)
 
     operate(0, 2, True)
@@ -495,7 +536,7 @@
     schur, local_inverse, rhs_parts, basis, coarse_map, coarse_inverse, shared_rows, shared_counts
 ):
     vmem = pl.BlockSpec(memory_space=pltpu.VMEM)
-    in_hbm = pl.BlockSpec(memory_space=pl.ANY)
+    in_hbm = pl.BlockSpec(memory_space=pltpu.HBM)
     dma = pltpu.SemaphoreType.DMA
     ar_shapes = [r // N_GROUP for r in AR_ROWS]
     scratch = [
@@ -511,8 +552,11 @@
         pltpu.VMEM((NL, NR), F32),
         pltpu.VMEM((NL, NR), F32),
         pltpu.VMEM((6, NL, NR), F32),
+        pltpu.VMEM((6, NL, NR), jnp.int16),
+        pltpu.VMEM((6, 4, 8, NR), F32),
+        pltpu.VMEM((6, 4, 8, NR), F32),
         pltpu.VMEM((4, ZONE, NR), BF),
-        pltpu.VMEM((6, 4, ZONE, NR), F32),
+        pltpu.VMEM((6, 4, ZONE, NR), jnp.int16),
         pltpu.VMEM((NL, NR), F32),
         pltpu.VMEM((4, NL, 2 * NR), BF),
         pltpu.VMEM((3, NL, 2 * NR), BF),
@@ -533,6 +577,8 @@
         pltpu.VMEM((4, NC, ZONE), BF),
         pltpu.VMEM((2, 4, NC, NR), F32),
         pltpu.VMEM((2, 4, NC, NR), F32),
+        pltpu.VMEM((10 * NC, NL), BF),
+        pltpu.VMEM((NC, NR), F32),
         pltpu.VMEM((3, NC, NR), F32),
         pltpu.VMEM((3, 4, NC, NR), F32),
         [pltpu.VMEM((r, NR), F32) for r in AR_ROWS],
@@ -564,6 +610,8 @@
         dma((2,)),
         dma((3,)),
         dma((3,)),
+        dma((6,)),
+        dma((6,)),
     ]
     out = jax.ShapeDtypeStruct((NL, NR), F32)
     x, r = pl.pallas_call(
@@ -573,12 +621,17 @@
         out_specs=(vmem, vmem),
         scratch_shapes=scratch,
         compiler_params=pltpu.CompilerParams(
-            collective_id=0, has_side_effects=True, vmem_limit_bytes=62 * 1024 * 1024
+            collective_id=0, has_side_effects=True, vmem_limit_bytes=40 * 1024 * 1024
         ),
         name="block_cg",
     )(
-        schur[0, 0], local_inverse[0, 0], rhs_parts[0, 0], basis[0, 0], coarse_map[0],
-        coarse_inverse[0], shared_rows[0, 0], shared_counts[0],
+        *[
+            pltpu.with_memory_space_constraint(a, pltpu.HBM)
+            for a in (
+                schur[0, 0], local_inverse[0, 0], rhs_parts[0, 0], basis[0, 0], coarse_map[0],
+                coarse_inverse[0], shared_rows[0, 0], shared_counts[0],
+            )
+        ]
     )
     return x[None, None], r[None, None]
 

time: 97.4 us -> 91.4 us (0.938)
  Pallas kernels: 92.8 us -> 89.1 us
  local copies, waits for them, and re-layouts: 3.74 us -> 1.59 us
    pallas_call x1, Pallas kernels: 92.8 us -> 89.1 us  [shards(): pl.pallas_call(kernel, out_shape=(out, out), in_specs=[in_hbm] * 8, out_s...]
    unnamed x2, local copies, waits for them, and re-layouts: 3.74 us -> 1.59 us
where the time goes in v4:
time: 91.4 us; the launch traced here: 91.3 us
  Pallas kernels  89.1 us (97%)
  local copies, waits for them, and re-layouts  1.59 us (2%)
    pallas_call x1, Pallas kernels, shards(): pl.pallas_call(kernel, out_shape=(out, out), in_specs=[in_hbm] * 8, out_s...  89.1 us

profile of v4, /device:TPU:1, one launch (start us, length us, event | category | flops | bytes accessed | tf_op | source)
XLA Modules:
  0.0 91.3 jit_solution(17916640578155052311)
XLA Ops:
  0.6 89.1 %block_cg.1 = (f32[1024,128]{1,0:T(8,128)S(1)}, f32[1024,128]{1,0:T(8,128)S(1)}) custom-call(bf16[1024,1024]{1,0:T(8,128)(2,1)} %bitcast.12, bf16[1024,1024]{1,0:T(8,128)(2,1)} %bitcast.13, bf16[1024,128]{1,0:T(8,128)(2,1)} %bitcast.14, bf16[32,1024]{1,0:T(8,128)(2,1)} %bitcast.16, s32[1,32]{1,0:T(1,128)} %bitcast.18, bf16[64,1024]{1,0:T(8,128)(2,1)} %bitcast.15, ...), custom_call_target="tpu_custom_call" | custom-call | tf_op jit(solution)/shard_map/block_cg/pallas_call | solution.py:617
  89.7 0.8 copy.12
  90.5 0.8 copy.13

commit v5 on v4

--- a/solution.py
+++ b/solution.py
@@ -132,7 +132,7 @@
 def kernel(
     schur_h, linv_h, rhs_h, basis_h, cmap_h, cinv_h, rows_h, counts_h,
     x_out, r_out,
-    schur, linv, rhs, basis, cmap, cinv, rows, counts, perm, weight, mult, sent, coded, step_mine, step_all, got0, got, r0, xw, xz, loc, base,
+    schur, linv, rhs, basis, cmap, cinv, rows, counts, perm, weight, mult, sent, coded, step_mine, step_all, got0, got, r0, xw, xz, loc,
     cl_mine, cl_all, map_mine, map_all, hot, e_mine, e_all, coarse, mat, top, bottom, g_mine, g_all, ct_mine, ct_all, gs_rows, own_share, pk_mine, pk_all,
     ar_in, ar_r1, ar_p, ar_r2, ar_q, ar_out,
     load_sem, xs, xr, cs, cr, ms, mr, es, er, as1, ar1, as2, ar2, as3, ar3, as4, ar4, gs, gr, ts, tr, ps, pr, qs, qr,
@@ -404,7 +404,7 @@
         total = ar_r1[i][0]
         for k in range(1, N_GROUP):
             total = total + ar_r1[i][k]
-        if i == 3:
+        if i in (1, 2, 3):
             return reduce_spread(i, 0, total, mates, as2, ar2)
         return reduce_spread(i, 1, total, mates_y, as2, ar2)
 
@@ -413,7 +413,7 @@
 
     def reduce_last(i, waits):
         share = AR_ROWS[i] // N_GROUP
-        total = reduce_sum(i, 0, waits, N_SUB) if i == 3 else reduce_sum(i, 2, waits, 4)
+        total = reduce_sum(i, 0, waits, N_SUB) if i in (1, 2, 3) else reduce_sum(i, 2, waits, 4)
         ar_q[i][...] = total
         mine = pl.ds(pl.multiple_of(share * g, 8), share)
         ar_out[i][mine, :] = total
@@ -456,29 +456,27 @@
     local_part(2, 5)
     ar_in[1][NR:, :] = gram(xz[1], xw[2])
     ar_b = reduce_start(1)
+    values_sent = coarse_part(2, 5, gathered)
     reduce_wait(ar_a)
     mat[0] = sym(ar_out[0][NR:, :])
     invert_lead(top.at[0], mat.at[0])
-    invert_steps(top.at[0], 0, 32)
-    values_sent = coarse_part(2, 5, gathered)
     ar_b = reduce_middle(1, ar_b)
-    invert_steps(top.at[0], 32, 64)
-    invert_next(top.at[0], bottom.at[0], mat.at[0])
     finish_z(2, 5, values_sent)
 
     operate(2, 6, False)
     ar_in[2][...] = gram(xz[2], xw[2])
     ar_c = reduce_start(2)
-    ar_b = reduce_more(1, ar_b)
-    invert_steps(bottom.at[0], 0, 64)
-    inv1 = invert_end(top.at[0], bottom.at[0])
-    m0 = ar_out[0][0:NR, :]
+    invert_steps(top.at[0], 0, 64)
+    invert_next(top.at[0], bottom.at[0], mat.at[0])
     ar_b = reduce_last(1, ar_b)
-    t0 = small(inv1, m0)
     finish_q(2, 6)
     ar_in[3][...] = gram(xz[2], xw[3])
     ar_d = reduce_start(3)
     ar_c = reduce_middle(2, ar_c)
+    invert_steps(bottom.at[0], 0, 64)
+    inv1 = invert_end(top.at[0], bottom.at[0])
+    m0 = ar_out[0][0:NR, :]
+    t0 = small(inv1, m0)
     reduce_wait(ar_b)
     m2 = sym(ar_out[1][0:NR, :])
     m3 = sym(ar_out[1][NR:, :])
@@ -486,7 +484,6 @@
     mat[1] = sym(m3 - small(m2, t2))
     invert_lead(top.at[1], mat.at[1])
     ar_d = reduce_middle(3, ar_d)
-    ar_c = reduce_more(2, ar_c)
     invert_steps(top.at[1], 0, 64)
     invert_next(top.at[1], bottom.at[1], mat.at[1])
     ar_c = reduce_last(2, ar_c)
@@ -505,16 +502,6 @@
     part = small(m3, t3) + small_t(s23, y)
     a0 = t0 - small(t2, u1)
     d0 = small(t2, y) - t3
-    x_out[...] = combine(xz[0], a0) + combine(xz[1], u1)
-    xd = xz[2]
-    base[0] = split(
-        xd[:, :NR].astype(F32) + xd[:, NR:].astype(F32) - combine(xz[1], y) + combine(xz[0], d0)
-    )
-    r_out[...] = r0[...] - mult[...] * (combine(xw[1], a0) + combine(xw[2], u1))
-    qd = xw[3]
-    base[1] = split(
-        qd[:, :NR].astype(F32) + qd[:, NR:].astype(F32) - combine(xw[2], y) + combine(xw[1], d0)
-    )
     reduce_wait(ar_d)
     mat[2] = sym(ar_out[3][...] - part)
     invert_lead(top.at[2], mat.at[2])
@@ -526,8 +513,10 @@
     invert_steps(bottom.at[2], 0, 64)
     below = small(bottom[2, :, :HALF], below)
     c2 = jnp.concatenate([above - small(cross, below), below], axis=0)
-    x_out[...] = x_out[...] + combine(base[0], c2)
-    r_out[...] = r_out[...] - mult[...] * combine(base[1], c2)
+    c1 = u1 - small(y, c2)
+    c0 = a0 + small(d0, c2)
+    x_out[...] = combine(xz[0], c0) + combine(xz[1], c1) + combine(xz[2], c2)
+    r_out[...] = r0[...] - mult[...] * (combine(xw[1], c0) + combine(xw[2], c1) + combine(xw[3], c2))
     for span, sem in started:
         arrived(span, sem)
 
@@ -561,7 +550,6 @@
         pltpu.VMEM((4, NL, 2 * NR), BF),
         pltpu.VMEM((3, NL, 2 * NR), BF),
         pltpu.VMEM((NL, NR), F32),
-        pltpu.VMEM((2, NL, 2 * NR), BF),
         pltpu.VMEM((3, NC, NR), F32),
         pltpu.VMEM((3, N_SUB, NC, NR), F32),
         pltpu.VMEM((8, NR), jnp.int32),

time: 91.4 us -> 89 us (0.974)
  Pallas kernels: 89.1 us -> 86.6 us
    pallas_call x1, Pallas kernels: 89.1 us -> 86.6 us  [shards(): pl.pallas_call(kernel, out_shape=(out, out), in_specs=[in_hbm] * 8, out_s...]
where the time goes in v5:
time: 89 us; the launch traced here: 88.9 us
  Pallas kernels  86.6 us (97%)
  local copies, waits for them, and re-layouts  1.59 us (2%)
    pallas_call x1, Pallas kernels, shards(): pl.pallas_call(kernel, out_shape=(out, out), in_specs=[in_hbm] * 8, out_s...  86.6 us

profile of v5, /device:TPU:1, one launch (start us, length us, event | category | flops | bytes accessed | tf_op | source)
XLA Modules:
  0.0 88.9 jit_solution(11365566695240471524)
XLA Ops:
  0.6 86.6 %block_cg.1 = (f32[1024,128]{1,0:T(8,128)S(1)}, f32[1024,128]{1,0:T(8,128)S(1)}) custom-call(bf16[1024,1024]{1,0:T(8,128)(2,1)} %bitcast.12, bf16[1024,1024]{1,0:T(8,128)(2,1)} %bitcast.13, bf16[1024,128]{1,0:T(8,128)(2,1)} %bitcast.14, bf16[32,1024]{1,0:T(8,128)(2,1)} %bitcast.16, s32[1,32]{1,0:T(1,128)} %bitcast.18, bf16[64,1024]{1,0:T(8,128)(2,1)} %bitcast.15, ...), custom_call_target="tpu_custom_call" | custom-call | tf_op jit(solution)/shard_map/block_cg/pallas_call | solution.py:605
  87.3 0.8 copy.12
  88.1 0.8 copy.13

commit v6 on v5

--- a/solution.py
+++ b/solution.py
@@ -199,24 +199,28 @@
         if d == 3:
             started.append((dst, xs.at[e]))
 
-    def ship(e, d, value):
-        sent[e - 1, zone(d), :] = value
-        top_value = jnp.maximum(jnp.max(jnp.abs(value), axis=0, keepdims=True), 2e-34)
-        step_mine[e - 1, d] = jnp.broadcast_to(top_value * (1.0 / 32767.0), (8, NR))
-        remote(
-            step_mine.at[e - 1, d], step_all.at[e - 1, d ^ 1], qs.at[e - 1], qr.at[e - 1], around[d]
-        )
-        if d == 3:
-            started.append((step_all.at[e - 1], qs.at[e - 1]))
-        steps = jnp.round(value * (32767.0 / top_value))
-        coded[e - 1, zone(d), :] = steps.astype(jnp.int32).astype(jnp.int16)
-        send_zone(e, d, coded.at[e - 1, zone(d)], got.at[e - 1])
+    def ship(e, zones, values):
+        tops = [
+            jnp.maximum(jnp.max(jnp.abs(v), axis=0, keepdims=True), 2e-34) for v in values
+        ]
+        steps = [jnp.round(v * (32767.0 / t)) for v, t in zip(values, tops)]
+        for d, value, top_value, codes in zip(zones, values, tops, steps):
+            sent[e - 1, zone(d), :] = value
+            step_mine[e - 1, d] = jnp.broadcast_to(top_value * (1.0 / 32767.0), (8, NR))
+            coded[e - 1, zone(d), :] = codes.astype(jnp.int32).astype(jnp.int16)
+        for d in zones:
+            remote(
+                step_mine.at[e - 1, d], step_all.at[e - 1, d ^ 1], qs.at[e - 1], qr.at[e - 1],
+                around[d],
+            )
+            send_zone(e, d, coded.at[e - 1, zone(d)], got.at[e - 1])
+            if d == 3:
+                started.append((step_all.at[e - 1], qs.at[e - 1]))
 
     def steps_arrived(e):
         arrived(step_all.at[e - 1], qr.at[e - 1])
 
     def shipped(e, d):
-        zone_arrived(e, d)
         steps = got[e - 1, d].astype(jnp.int32).astype(F32)
         return fold(dot(perm[d], split(steps))) * step_all[e - 1, d, 0:1, :]
 
@@ -252,11 +256,14 @@
         [(g_mine.at[d], g_all.at[d ^ 1], around[d]) for d in range(4)], g_all, gs.at[0], gr.at[0]
     )
 
-    for d in (2, 3, 0, 1):
-        zone_arrived(0, d)
-        block = rhs[zone(d), :].astype(F32) + dot(perm[d], got0[d])
-        r0[zone(d), :] = block
-        xw[0, zone(d), :] = split(weight[zone(d), :] * block)
+    for zones in ((2, 3), (0, 1)):
+        for d in zones:
+            zone_arrived(0, d)
+        whole = [rhs[zone(d), :].astype(F32) + dot(perm[d], got0[d]) for d in zones]
+        halves = [split(weight[zone(d), :] * v) for d, v in zip(zones, whole)]
+        for d, value, pair in zip(zones, whole, halves):
+            r0[zone(d), :] = value
+            xw[0, zone(d), :] = pair
 
     def coarse_send(k, local):
         cl_mine[k] = local
@@ -300,8 +307,8 @@
 
     def local_part(k, e):
         blocks = xw[k]
-        for d in range(4):
-            ship(e, d, weight[zone(d), :] * local_apply(linv, blocks, d))
+        for zones in ((0, 1), (2, 3)):
+            ship(e, zones, [weight[zone(d), :] * local_apply(linv, blocks, d) for d in zones])
 
     def coarse_part(k, e, gathered):
         arrived(*gathered)
@@ -320,11 +327,16 @@
 
     def finish_z(k, e, values_sent):
         arrived(*values_sent)
+        for d in range(4):
+            theirs = fold(dot(g_all[d], split(pk_all[k, d]), ((0,), (0,))))
+            loc[zone(d), :] = loc[zone(d), :] + theirs
         steps_arrived(e)
-        for d in (2, 3, 0, 1):
-            theirs = fold(dot(g_all[d], split(pk_all[k, d]), ((0,), (0,))))
-            mine = loc[zone(d), :] + theirs
-            xz[k, zone(d), :] = split(mine + shipped(e, d))
+        for zones in ((2, 3), (0, 1)):
+            for d in zones:
+                zone_arrived(e, d)
+            whole = [split(loc[zone(d), :] + shipped(e, d)) for d in zones]
+            for d, value in zip(zones, whole):
+                xz[k, zone(d), :] = value
 
     def shares_setup():
         row = lax.broadcasted_iota(jnp.int32, (ZONE, ZONE), 0)
@@ -355,8 +367,8 @@
                 remote(ct_mine.at[k, d], ct_all.at[k, d ^ 1], ts.at[k], tr.at[k], around[d])
             started.append((ct_all.at[k], ts.at[k]))
             own_share[...] = terms[4]
-        for d in range(4):
-            ship(e, d, local_apply(schur, blocks, d))
+        for zones in ((0, 1), (2, 3)):
+            ship(e, zones, [local_apply(schur, blocks, d) for d in zones])
 
     def coarse_shares(k, e):
         total = own_share[...]
@@ -367,9 +379,14 @@
 
     def finish_q(k, e):
         steps_arrived(e)
-        for d in (2, 3, 0, 1):
-            whole = sent[e - 1, zone(d), :] + shipped(e, d)
-            xw[k + 1, zone(d), :] = split(weight[zone(d), :] * whole)
+        for zones in ((2, 3), (0, 1)):
+            for d in zones:
+                zone_arrived(e, d)
+            whole = [
+                split(weight[zone(d), :] * (sent[e - 1, zone(d), :] + shipped(e, d))) for d in zones
+            ]
+            for d, value in zip(zones, whole):
+                xw[k + 1, zone(d), :] = value
 
     def reduce_start(i):
         share = AR_ROWS[i] // N_GROUP

time: 89 us -> 85.8 us (0.964)
  Pallas kernels: 86.6 us -> 83.5 us
    pallas_call x1, Pallas kernels: 86.6 us -> 83.5 us  [shards(): pl.pallas_call(kernel, out_shape=(out, out), in_specs=[in_hbm] * 8, out_s...]
where the time goes in v6:
time: 85.8 us; the launch traced here: 85.7 us
  Pallas kernels  83.5 us (97%)
  local copies, waits for them, and re-layouts  1.59 us (2%)
    pallas_call x1, Pallas kernels, shards(): pl.pallas_call(kernel, out_shape=(out, out), in_specs=[in_hbm] * 8, out_s...  83.5 us

profile of v6, /device:TPU:1, one launch (start us, length us, event | category | flops | bytes accessed | tf_op | source)
XLA Modules:
  0.0 85.7 jit_solution(716232911409573259)
XLA Ops:
  0.6 83.5 %block_cg.1 = (f32[1024,128]{1,0:T(8,128)S(1)}, f32[1024,128]{1,0:T(8,128)S(1)}) custom-call(bf16[1024,1024]{1,0:T(8,128)(2,1)} %bitcast.12, bf16[1024,1024]{1,0:T(8,128)(2,1)} %bitcast.13, bf16[1024,128]{1,0:T(8,128)(2,1)} %bitcast.14, bf16[32,1024]{1,0:T(8,128)(2,1)} %bitcast.16, s32[1,32]{1,0:T(1,128)} %bitcast.18, bf16[64,1024]{1,0:T(8,128)(2,1)} %bitcast.15, ...), custom_call_target="tpu_custom_call" | custom-call | tf_op jit(solution)/shard_map/block_cg/pallas_call | solution.py:622
  84.1 0.8 copy.12
  84.9 0.8 copy.13
